TPU v7x, 512 devices: a whole 4x4x16 slice. The times are simulated.
512 devices in a mesh: batch: 16 (over z_hi, x), tm: 32 (over y, z_lo, core).
Axes of the slice: x: 4, y: 4, z: 16 (z_hi: 4, z_lo: 4; z = z_hi * 4 + z_lo), core: 2. Of those that a mesh axis runs over, the one named last changes fastest.
Arguments:
- raw: bfloat16 [16, 4096, 640], P('batch', 'tm'), may hold values from -6 to 6
- w_conv: bfloat16 [1280, 512], replicated, may hold values from -0.15625 to 0.15625
- w_query: bfloat16 [512, 1024], replicated, may hold values from -0.25 to 0.25
- w_key: bfloat16 [512, 1024], replicated, may hold values from -0.25 to 0.25
- w_pred: bfloat16 [2, 512, 512], replicated, may hold values from -0.25 to 0.25
- log_decay: float32 [16, 8, 4096], P('batch', None, 'tm'), may hold values from -1 to 0
- lengths: int32 [16], P('batch'), may hold values from 2048 to 4096, as said below
- neg_offset: int32 [16, 4096, 3], P('batch', 'tm'), may hold values from 0 to 14, all different within a row; in each aligned block of 128 rows (0 to 127, 128 to 255, ..., all dimensions but the last counted through in order) at most 39 rows name the same one
- neg_frame: int32 [16, 4096, 3], P('batch', 'tm'), may hold values from 0 to 127
Outputs:
- logits: float32 [16, 2, 4, 4096], P('batch', None, None, 'tm')
Inputs may be any that keep to these rules, and one draw needn't show every extreme that they name: `neg_offset`: in each device's 128 frames (an aligned block of rows), a frame's 3 offsets are distinct, and no offset is named by more than 39 of those frames; some offset is named by exactly 39 of them. `neg_frame`: a frame of the anchor's own time shard of 128 frames. `lengths`: one stream holds all 4096 frames and another exactly half of them.
All inputs are finite; a program needn't handle non-finite values.
Results may differ from a plain program's by a relative error of at most 0.0094.
Values may be sent and summed in bfloat16 or wider, within the bound.
A program may use at most 64 MiB of HBM per device.

v0:
```python
import math

import jax
import jax.numpy as jnp
from jax import lax
from jax.sharding import PartitionSpec as P

SPAN = 128


def passed_along(value, axis, steps):
    count = lax.axis_size(axis)
    leading, last = (max(0, -steps), min(count, count - steps))
    return lax.ppermute(value, axis, [(source, source + steps) for source in range(leading, last)])


def carried_in(value, axis, join, neutral):
    count, mine = (lax.axis_size(axis), lax.axis_index(axis))
    pieces = jax.tree.map(lambda part: lax.all_gather(part, axis), value)
    subtotal = jax.tree.map(
        lambda part, zero: jnp.full_like(part, 0) + jnp.asarray(zero, part.dtype), value, neutral
    )

    def turn(position, subtotal):
        longer = join(subtotal, jax.tree.map(lambda part: part[position], pieces))
        return jax.tree.map(lambda new, old: jnp.where(position < mine, new, old), longer, subtotal)

    return lax.fori_loop(0, count - 1, turn, subtotal)


def rms_rows(values):
    return values * lax.rsqrt(jnp.mean(values * values, axis=-1, keepdims=True) + 1e-05)


def shards(raw, w_conv, w_query, w_key, w_pred, log_decay, lengths, neg_offset, neg_frame):
    frames_dev = raw.shape[1]
    width_in = raw.shape[2]
    channels = w_conv.shape[1]
    heads = log_decay.shape[1]
    head_key = w_query.shape[1] // heads
    head_value = channels // heads
    steps_ahead = w_pred.shape[0]
    block_len = SPAN
    n_blocks = frames_dev // block_len
    cycle_size = lax.axis_size("batch")
    my_group = lax.axis_index("batch")
    position = lax.axis_index("tm") * frames_dev + jnp.arange(frames_dev, dtype=jnp.int32)
    signal = raw[0]
    last_frame = passed_along(signal[-1:], "tm", 1)
    earlier = jnp.concatenate([last_frame, signal[:-1]], axis=0)
    hidden = jnp.dot(earlier, w_conv[:width_in], preferred_element_type=jnp.float32)
    hidden = hidden + jnp.dot(signal, w_conv[width_in:], preferred_element_type=jnp.float32)
    valid_mask = (position < lengths[0]).astype(jnp.float32)
    encoded = (rms_rows(jax.nn.gelu(hidden)) * valid_mask[:, None]).astype(jnp.bfloat16)
    future = passed_along(encoded[:steps_ahead], "tm", -1)
    queries = jnp.dot(encoded, w_query, preferred_element_type=jnp.float32).astype(jnp.bfloat16)
    key_rows = jnp.dot(encoded, w_key, preferred_element_type=jnp.float32).astype(jnp.bfloat16)
    queries = queries.reshape(n_blocks, block_len, heads, head_key)
    key_rows = key_rows.reshape(n_blocks, block_len, heads, head_key)
    values = encoded.reshape(n_blocks, block_len, heads, head_value)
    decay_rates = jnp.transpose(log_decay[0].reshape(heads, n_blocks, block_len), (1, 0, 2))
    log_cum = jnp.cumsum(decay_rates, axis=-1)
    totals = log_cum[:, :, -1]
    to_end = jnp.transpose(jnp.exp(totals[:, :, None] - log_cum), (0, 2, 1))
    weighted = (key_rows.astype(jnp.float32) * to_end[..., None]).astype(jnp.bfloat16)
    updates = jnp.einsum("jshd,jshe->jhde", weighted, values, preferred_element_type=jnp.float32)

    def advance(running, item):
        total, update = item
        return (jnp.exp(total)[:, None, None] * running + update, running)

    zero_state = jnp.zeros((heads, head_key, head_value), jnp.float32)
    local_state, _ = lax.scan(advance, zero_state, (totals, updates))
    local_decay = jnp.exp(jnp.sum(totals, axis=0))

    def combine(earlier_pair, later_pair):
        return (
            earlier_pair[0] * later_pair[0],
            later_pair[0][:, None, None] * earlier_pair[1] + later_pair[1],
        )

    incoming = carried_in(
        (local_decay, local_state), "tm", combine, (jnp.ones((heads,), jnp.float32), zero_state)
    )
    _, entries = lax.scan(advance, incoming[1], (totals, updates))
    scale = 1.0 / math.sqrt(head_key)
    causal = jnp.arange(block_len)[:, None] >= jnp.arange(block_len)[None, :]
    scores = jnp.einsum("jthd,jshd->jhts", queries, key_rows, preferred_element_type=jnp.float32)
    log_gap = log_cum[:, :, :, None] - log_cum[:, :, None, :]
    weight = jnp.where(causal, jnp.exp(jnp.minimum(log_gap, 0.0)), 0.0)
    weights_bf = (scores * weight * scale).astype(jnp.bfloat16)
    inside = jnp.einsum("jhts,jshe->jthe", weights_bf, values, preferred_element_type=jnp.float32)
    carried = jnp.einsum(
        "jthd,jhde->jthe", queries, entries.astype(jnp.bfloat16), preferred_element_type=jnp.float32
    )
    carried = carried * jnp.transpose(jnp.exp(log_cum) * scale, (0, 2, 1))[..., None]
    attended = (inside + carried).reshape(frames_dev, heads, head_value)
    context = rms_rows(attended).reshape(frames_dev, channels).astype(jnp.bfloat16)
    extended = jnp.concatenate([encoded, future], axis=0)
    target_group = (my_group + neg_offset[0] + 1) % cycle_size
    target_frame = neg_frame[0]
    everyone = lax.all_gather(encoded, "batch", axis=0, tiled=True)
    picked = everyone[target_group * frames_dev + target_frame]
    inv_width = 1.0 / math.sqrt(channels)
    step_rows = []
    for ahead_step in range(steps_ahead):
        predicted = jnp.dot(context, w_pred[ahead_step], preferred_element_type=jnp.float32).astype(
            jnp.bfloat16
        )
        targets = extended[ahead_step + 1 : ahead_step + 1 + frames_dev]
        positive = (
            jnp.einsum("te,te->t", predicted, targets, preferred_element_type=jnp.float32)
            * inv_width
        )
        negative = (
            jnp.einsum("te,tje->jt", predicted, picked, preferred_element_type=jnp.float32)
            * inv_width
        )
        step_rows.append(jnp.concatenate([positive[None, :], negative], axis=0))
    logits = jnp.stack(step_rows, axis=0) * valid_mask[None, None, :]
    return logits[None]


def solution(mesh):
    placed = (
        P("batch", "tm", None),
        P(),
        P(),
        P(),
        P(),
        P("batch", None, "tm"),
        P("batch"),
        P("batch", "tm", None),
        P("batch", "tm", None),
    )
    return jax.shard_map(
        shards, mesh=mesh, in_specs=placed, out_specs=P("batch", None, None, "tm"), check_vma=False
    )
```

profile of v0, /device:TPU:1, one launch (start us, length us, event | category | flops | bytes accessed | tf_op | source)
XLA Modules:
  0.0 259.7 jit_solution(6791803627788913415)
XLA Ops:
  7.4 4.9 %collective-permute-start = (bf16[1,640]{1,0:T(2,128)(2,1)S(1)}, bf16[1,640]{1,0:T(2,128)(2,1)S(1)}, u32[]{:S(2)}, u32[]{:S(2)}) collective-permute-start(bf16[1,640]{1,0:T(2,128)(2,1)S(1)} %slice_bitcast_fusion.1), channel_id=1, source_target_pairs={{0,1},{1,2},{2,3},{3,4},{4,5},{5,6},{6,7},{7,8},{8,9},{9,10},{10,1... | collective-permute-start | bytes 3848 | tf_op jit(solution)/shard_map/ppermute | solution.py:14
  13.9 1.4 fusion.9
  18.0 1.1 copy.24
  19.1 1.3 fusion.5
  20.4 1.1 convolution_add_fusion
  21.9 44.0 %all-gather = f32[32,8,1]{1,2,0:T(1,128)} all-gather(f32[1,8,1]{1,2,0:T(1,128)S(1)} %copy.27), channel_id=2, replica_groups=mesh['batch'=16,'tm'=32] {'tm'}, dimensions={0}, use_global_device_ids=true | all-gather | bytes 1056 | tf_op jit(solution)/shard_map/all_gather | solution.py:19
  66.0 2.1 collective-permute-start.1
  68.9 46.5 %all-gather.5.cloned.1.call-done = bf16[2048,512]{1,0:T(8,128)(2,1)} async-done(((bf16[128,512]{1,0:T(8,128)(2,1)}), bf16[2048,512]{1,0:T(8,128)(2,1)}) %all-gather.5.cloned.1.call-update) | async-done | bytes 2097168 | tf_op jit(solution)/shard_map/all_gather | solution.py:102
  115.4 3.9 %gather_fusion = bf16[384,512]{1,0:T(8,128)(2,1)S(1)} fusion(bf16[2048,512]{1,0:T(8,128)(2,1)} %all-gather.5.cloned.1.call-done, s32[1024]{0:T(1024)S(1)} %pad_clamp_fusion), kind=kCustom, calls=%fused_computation | custom fusion | bytes 787968 | tf_op jit(solution)/shard_map/gather | solution.py:103
  119.6 66.6 %all-gather.7.cloned.1.call-done = f32[256,128,64]{1,2,0:T(8,128)} async-done(((f32[8,128,64]{1,2,0:T(8,128)}), f32[256,128,64]{1,2,0:T(8,128)}) %all-gather.7.cloned.1.call-update) | async-done | bytes 8388624 | tf_op jit(solution)/shard_map/all_gather | solution.py:19
  186.3 62.9 %while.9 = (s32[]{:T(128)}, f32[8,128,64]{2,1,0:T(8,128)S(1)}, s32[]{:T(128)}, f32[32,8]{1,0:T(8,128)}, f32[32,8,128,64]{2,3,1,0:T(8,128)}, /*index=5*/s32[]{:T(128)}, s32[]{:T(128)}) while((s32[]{:T(128)}, f32[8,128,64]{2,1,0:T(8,128)S(1)}, s32[]{:T(128)}, f32[32,8]{1,0:T(8,128)}, f32[32,8,128,64]{2,3,1,0:T(8,128)}, ...), condition=%wide.region_3.4_spmd.clone, body=%wide.region_2.3_spmd.clone.sunk | while | flops 262148 | bytes 1835209 | solution.py:28
  186.3 1.0 constant_dynamic-slice_fusion.2
  188.3 1.0 constant_dynamic-slice_fusion.2
  190.3 1.0 constant_dynamic-slice_fusion.2
  192.4 1.0 constant_dynamic-slice_fusion.2
  194.4 1.0 constant_dynamic-slice_fusion.2
  196.4 1.0 constant_dynamic-slice_fusion.2
  198.4 1.0 constant_dynamic-slice_fusion.2
  200.5 1.0 constant_dynamic-slice_fusion.2
  202.5 1.0 constant_dynamic-slice_fusion.2
  204.5 1.0 constant_dynamic-slice_fusion.2
  206.5 1.0 constant_dynamic-slice_fusion.2
  208.6 1.0 constant_dynamic-slice_fusion.2
  210.6 1.0 constant_dynamic-slice_fusion.2
  212.6 1.0 constant_dynamic-slice_fusion.2
  214.7 1.0 constant_dynamic-slice_fusion.2
  216.7 1.0 constant_dynamic-slice_fusion.2
  218.7 1.0 constant_dynamic-slice_fusion.2
  220.8 1.0 constant_dynamic-slice_fusion.2
  224.8 1.0 constant_dynamic-slice_fusion.2
  226.8 1.0 constant_dynamic-slice_fusion.2
  245.1 1.0 constant_dynamic-slice_fusion.2
  (165 shorter events, 51.1 us)
Async XLA Ops:
  6.5 12.5 %copy-start = (bf16[512,1024]{1,0:T(8,128)(2,1)S(1)}, bf16[512,1024]{1,0:T(8,128)(2,1)}, u32[]{:S(2)}) copy-start(bf16[512,1024]{1,0:T(8,128)(2,1)} %param.14) | copy-start | bytes 3145732
  6.5 9.6 %copy-start.5 = (bf16[1280,512]{1,0:T(8,128)(2,1)S(1)}, bf16[1280,512]{1,0:T(8,128)(2,1)}, u32[]{:S(2)}) copy-start(bf16[1280,512]{1,0:T(8,128)(2,1)} %param.12) | copy-start | bytes 3932164
  6.5 108.9 %all-gather.5.cloned.1.call-start = ((), (), s32[]{:S(2)}) async-start(), calls=%async_computation | async-start | bytes 2228224 | tf_op jit(solution)/shard_map/all_gather | solution.py:102
  7.4 8.8 %collective-permute-start = (bf16[1,640]{1,0:T(2,128)(2,1)S(1)}, bf16[1,640]{1,0:T(2,128)(2,1)S(1)}, u32[]{:S(2)}, u32[]{:S(2)}) collective-permute-start(bf16[1,640]{1,0:T(2,128)(2,1)S(1)} %slice_bitcast_fusion.1), channel_id=1, source_target_pairs={{0,1},{1,2},{2,3},{3,4},{4,5},{5,6},{6,7},{7,8},{8,9},{9,10},{10,1... | collective-permute-start | bytes 3848 | tf_op jit(solution)/shard_map/ppermute | solution.py:14
  15.4 2.1 copy-start.7
  17.4 168.9 %all-gather.7.cloned.1.call-start = ((), (), s32[]{:S(2)}) async-start(), calls=%async_computation.1 | async-start | bytes 8650752 | tf_op jit(solution)/shard_map/all_gather | solution.py:19
  18.0 3.6 %copy-start.8 = (s32[1,128,3]{1,0,2:T(1,128)S(1)}, s32[1,128,3]{1,0,2:T(1,128)}, u32[]{:S(2)}) copy-start(s32[1,128,3]{1,0,2:T(1,128)} %param.19) | copy-start | bytes 4612
  18.0 3.6 %copy-start.9 = (s32[1,128,3]{1,0,2:T(1,128)S(1)}, s32[1,128,3]{1,0,2:T(1,128)}, u32[]{:S(2)}) copy-start(s32[1,128,3]{1,0,2:T(1,128)} %param.18) | copy-start | bytes 4612
  19.1 46.9 %copy-start.1 = (bf16[128,512]{1,0:T(8,128)(2,1)S(1)}, bf16[128,512]{1,0:T(8,128)(2,1)}, u32[]{:S(2)}) copy-start(bf16[128,512]{1,0:T(8,128)(2,1)} %multiply_convert_fusion.3) | copy-start | bytes 393220
  19.1 49.0 %copy-start.2 = (bf16[512,1024]{1,0:T(8,128)(2,1)S(1)}, bf16[512,1024]{1,0:T(8,128)(2,1)}, u32[]{:S(2)}) copy-start(bf16[512,1024]{1,0:T(8,128)(2,1)} %param.13) | copy-start | bytes 3145732
  66.0 184.6 %collective-permute-start.1 = (bf16[2,512]{1,0:T(2,128)(2,1)S(1)}, bf16[2,512]{1,0:T(2,128)(2,1)S(1)}, u32[]{:S(2)}, u32[]{:S(2)}) collective-permute-start(bf16[2,512]{1,0:T(2,128)(2,1)S(1)} %slice.50), channel_id=1, source_target_pairs={{1,0},{2,1},{3,2},{4,3},{5,4},{6,5},{7,6},{8,7},{9,8},{10,9},{11,1... | collective-permute-start | bytes 6152 | tf_op jit(solution)/shard_map/ppermute | solution.py:14
  68.4 51.0 %copy-start.3 = (bf16[16,8,8,128]{3,2,1,0:T(8,128)(2,1)}, bf16[16,8,8,128]{3,2,1,0:T(8,128)(2,1)S(1)}, u32[]{:S(2)}) copy-start(bf16[16,8,8,128]{3,2,1,0:T(8,128)(2,1)S(1)} %fusion.4) | copy-start | bytes 786436
  186.3 62.9 %copy-start.4 = (bf16[16,8,8,128]{3,2,1,0:T(8,128)(2,1)S(1)}, bf16[16,8,8,128]{3,2,1,0:T(8,128)(2,1)}, u32[]{:S(2)}) copy-start(bf16[16,8,8,128]{3,2,1,0:T(8,128)(2,1)} %copy-done.3) | copy-start | bytes 786436
  249.1 1.2 copy-start.6
Sparse Core Ops, SparseCore 0:
  17.5 97.8 all-gather.4
  117.6 68.6 all-gather.6
where the time goes:
time: 262 us; the launch traced here: 260 us
  waiting for transfers between devices  114 us (44%)
  local copies, waits for them, and re-layouts  66.4 us (25%)
  blocking collectives  44 us (17%)
  between operations  14.3 us (5%)
  matrix products  7.05 us (3%)
  starting transfers between devices  7.03 us (3%)
  other arithmetic  6.05 us (2%)
    all_gather x1, waiting for transfers between devices, carried_in(): pieces = jax.tree.map(lambda part: lax.all_gather(part, axis), value)  66.6 us
    all_gather x1, waiting for transfers between devices, shards(): everyone = lax.all_gather(encoded, 'batch', axis=0, tiled=True)  46.5 us
    all_gather x1, blocking collectives, carried_in(): pieces = jax.tree.map(lambda part: lax.all_gather(part, axis), value)  44 us
    dynamic_slice x62, local copies, waits for them, and re-layouts, turn(): longer = join(subtotal, jax.tree.map(lambda part: part[position], pieces))  36.4 us
    mul x31, local copies, waits for them, and re-layouts, combine(): later_pair[0][:, None, None] * earlier_pair[1] + later_pair[1]  21.4 us
    ppermute x2, starting transfers between devices, passed_along(): lax.ppermute(value, axis, [(source, source + steps) for source in range(l...  6.99 us
  transfers between devices with their start and end apart: 4, of which 3 were waited for; matrix products, arithmetic and copies ran while one was open for 29% of the time, Pallas kernels for 0%

commit v1 on v0

v1 whole, which is shorter than its diff:
```python
import functools
import math

import jax
import jax.numpy as jnp
from jax import lax
from jax.experimental import pallas as pl
from jax.experimental.pallas import tpu as pltpu
from jax.sharding import PartitionSpec as P

MESH = pl.DeviceIdType.MESH
F32, BF16, I32 = jnp.float32, jnp.bfloat16, jnp.int32
FD, E, DA, H, FRAME_W, K, NNEG = 128, 512, 1024, 8, 640, 2, 3
DK, DV = DA // H, E // H
SLOT = 48
HALF = FD // 2
MSG = DV + 16
YMSG = DV + 8


def nt(a, b):
    return lax.dot_general(a, b, (((1,), (1,)), ((), ())), preferred_element_type=F32)


def nn(a, b):
    return jnp.dot(a, b, preferred_element_type=F32)


def iota(shape, axis):
    return lax.broadcasted_iota(I32, shape, axis)


def kernel(
    raw_hbm, wc_hbm, wq_hbm, wk_hbm, wp_hbm, ld_hbm, aux_hbm, out_ref,
    raw, wc, wq, wk, wp, ld, aux, halo, fut, want, asked, grid, pick, rows,
    msg_out, msg_in, y_out, y_in, ent_out, ent, q_s, inside,
    load_sem, halo_sem, fut_sem, ask_sem, near_sem, far_sem, row_sem, msg_sem, y_sem, ent_sem,
):
    b, m = lax.axis_index("batch"), lax.axis_index("tm")
    zh, x = b // 4, b % 4
    y, i = m // 8, m % 8

    def at(zz=None, xx=None, tm=None):
        zz = zh if zz is None else zz
        xx = x if xx is None else xx
        return (zz * 4 + xx, m if tm is None else tm)

    def remote(src, dst, sems, index, dev):
        return pltpu.make_async_remote_copy(
            src_ref=src, dst_ref=dst, send_sem=sems.at[(0, *index)], recv_sem=sems.at[(1, *index)],
            device_id=dev, device_id_type=MESH,
        )

    z_up, z_dn = at(zz=(zh + 1) % 4), at(zz=(zh + 3) % 4)
    x_of = [at(xx=(x + d) % 4) for d in range(4)]
    row_of = [at(tm=y * 8 + (i + d) % 8) for d in range(8)]
    y_of = [at(tm=((y + d) % 4) * 8 + i) for d in range(4)]
    nxt, prv = at(tm=jnp.minimum(m + 1, 31)), at(tm=jnp.maximum(m - 1, 0))
    has_next, has_prev = m < 31, m > 0
    edge_next = jnp.logical_and(i == 7, has_next)
    edge_prev = jnp.logical_and(i == 0, has_prev)

    barrier = pltpu.get_barrier_semaphore()
    for dev in [z_up, z_dn] + x_of[1:] + row_of[1:] + y_of[1:]:
        pl.semaphore_signal(barrier, inc=1, device_id=dev, device_id_type=MESH)

    @pl.when(edge_next)
    def _():
        pl.semaphore_signal(barrier, inc=1, device_id=nxt, device_id_type=MESH)

    @pl.when(edge_prev)
    def _():
        pl.semaphore_signal(barrier, inc=1, device_id=prv, device_id_type=MESH)

    loads = [
        pltpu.make_async_copy(src, dst, load_sem.at[n])
        for n, (src, dst) in enumerate(
            [(raw_hbm.at[0], raw), (wc_hbm, wc), (aux_hbm, aux), (ld_hbm.at[0], ld),
             (wk_hbm, wk), (wq_hbm, wq), (wp_hbm, wp)]
        )
    ]
    for load in loads:
        load.start()

    loads[2].wait()
    lane = iota((FD, FD), 1)
    sub = iota((FD, FD), 0)
    rel_j, frame_j = [], []
    for j in range(NNEG):
        group = (b + aux[j : j + 1, :] + 1) & 15
        rel_j.append((((zh - (group >> 2)) & 3) << 2) | ((x - (group & 3)) & 3))
        frame_j.append(aux[3 + j : 4 + j, :])
    rel_rows = iota((16, FD), 0)
    hit = [jnp.where(rel_rows == rel_j[j], 1, 0) for j in range(NNEG)]
    named = hit[0] + hit[1] + hit[2]
    frame_of = hit[0] * frame_j[0] + hit[1] * frame_j[1] + hit[2] * frame_j[2]
    upto = jnp.where(sub <= lane, 1.0, 0.0).astype(BF16)
    rank = nn(named.astype(F32).astype(BF16), upto).astype(I32) - 1
    spot = [jnp.sum(hit[j] * (rel_rows * SLOT + rank), axis=0, keepdims=True) for j in range(NNEG)]
    code = jnp.where(named > 0, rank, -1)
    slot_rows = iota((SLOT, FD), 0)
    slot_lane = iota((SLOT, FD), 1)
    wanted = jnp.zeros((SLOT, FD), I32)
    for r in range(1, 16):
        column = jnp.sum(
            jnp.where(slot_rows == code[r : r + 1, :], frame_of[r : r + 1, :].astype(F32), 0.0), axis=1, keepdims=True
        )
        wanted = jnp.where(slot_lane == r, column.astype(I32), wanted)
    want[...] = wanted

    loads[3].wait()
    cum = ld[...]
    lane8 = iota((H, FD), 1)
    for shift in (1, 2, 4, 8, 16, 32, 64):
        cum = cum + jnp.where(lane8 >= shift, pltpu.roll(cum, shift, 1), 0.0)
    cum_col = jnp.concatenate([cum, jnp.zeros((FD - H, FD), F32)], axis=0).T
    total = jnp.sum(jnp.where(lane8 == FD - 1, cum, 0.0), axis=1, keepdims=True)
    total_row = jnp.broadcast_to(total, (H, FD))

    loads[0].wait()
    loads[1].wait()
    before = nn(raw[...], wc[:FRAME_W, :])
    now = nn(raw[...], wc[FRAME_W:, :])

    pl.semaphore_wait(barrier, 15 + jnp.where(edge_next, 1, 0) + jnp.where(edge_prev, 1, 0))
    halo_copy = remote(raw.at[pl.ds(FD - 16, 16), :], halo, halo_sem, (), nxt)

    @pl.when(has_next)
    def _():
        halo_copy.start()

    asks = [remote(want, asked.at[d], ask_sem, (d,), x_of[(4 - d) % 4]) for d in range(1, 4)]
    for copy in asks:
        copy.start()

    @pl.when(has_prev)
    def _():
        halo_copy.wait_recv()

    @pl.when(jnp.logical_not(has_prev))
    def _():
        halo[...] = jnp.zeros_like(halo)

    edge = nn(halo[...], wc[:FRAME_W, :])
    first = iota((FD, E), 0) == 0
    hidden = now + jnp.where(first, jnp.broadcast_to(edge[15:16, :], (FD, E)), pltpu.roll(before, 1, 0))
    u = jax.nn.gelu(hidden)
    normed = u * lax.rsqrt(jnp.mean(u * u, axis=-1, keepdims=True) + 1e-05)
    length = aux[6:7, :]
    valid_rows = jnp.where(sub + m * FD < length, 1.0, 0.0)
    enc = (normed * jnp.concatenate([valid_rows] * 4, axis=1)).astype(BF16)
    grid[0] = enc

    low, high = pl.ds(0, HALF), pl.ds(HALF, HALF)
    up = [remote(grid.at[0, part, :], grid.at[1, part, :], near_sem, (0, n), z_up) for n, part in enumerate((low, high))]
    dn = [remote(grid.at[0, part, :], grid.at[3, part, :], near_sem, (1, n), z_dn) for n, part in enumerate((high, low))]
    far_up = remote(grid.at[1, low, :], grid.at[2, low, :], far_sem, (0,), z_up)
    far_dn = remote(grid.at[3, high, :], grid.at[2, high, :], far_sem, (1,), z_dn)
    for n in range(2):
        up[n].start()
        dn[n].start()
    fut_copy = remote(grid.at[0, pl.ds(0, 16), :], fut, fut_sem, (), prv)

    @pl.when(has_prev)
    def _():
        fut_copy.start()

    loads[4].wait()
    enc_t = [enc[:, c * FD : (c + 1) * FD].T for c in range(E // FD)]
    value_t = [enc_t[h // 2][(h % 2) * DV : (h % 2 + 1) * DV, :] for h in range(H)]
    keys = nn(enc, wk[...]).astype(BF16)
    lane16 = iota((16, FD), 0)
    for h in range(H):
        key = keys[:, h * DK : (h + 1) * DK]
        to_end = jnp.exp(total_row[h : h + 1, :] - jnp.broadcast_to(cum_col[:, h : h + 1], (FD, FD)))
        weighted = (key.astype(F32) * to_end).astype(BF16)
        state = nn(value_t[h], weighted)
        msg_out[h, pl.ds(0, DV), :] = state.astype(BF16)
        whole = total_row[h : h + 1, :]
        hi = whole.astype(BF16).astype(F32)
        mid = (whole - hi).astype(BF16).astype(F32)
        lo = whole - hi - mid
        pieces = jnp.where(lane16 == 0, hi, jnp.where(lane16 == 1, mid, jnp.where(lane16 == 2, lo, 0.0)))
        msg_out[h, pl.ds(DV, 16), :] = pieces.astype(BF16)
    mine = pltpu.make_async_copy(msg_out.at[i], msg_in.at[i], load_sem.at[7])
    mine.start()
    msgs = [remote(msg_out.at[(i + d) % 8], msg_in.at[i], msg_sem, (d,), row_of[d]) for d in range(1, 8)]
    for copy in msgs:
        copy.start()

    loads[5].wait()
    queries = nn(enc, wq[...]).astype(BF16)
    q_s[...] = queries
    scale = 1.0 / math.sqrt(DK)
    for h in range(H):
        key = keys[:, h * DK : (h + 1) * DK]
        query = queries[:, h * DK : (h + 1) * DK]
        gap = cum[h : h + 1, :] - jnp.broadcast_to(cum_col[:, h : h + 1], (FD, FD))
        weight = jnp.where(sub <= lane, jnp.exp(jnp.minimum(gap, 0.0)), 0.0)
        probs_t = (nt(key, query) * weight * scale).astype(BF16)
        inside[h] = nn(value_t[h], probs_t)

    for copy in asks:
        copy.wait()

    def serve(dz):
        block = grid[dz]
        sends = []
        for d in range(4):
            if dz == 0 and d == 0:
                continue
            lists = want[...] if d == 0 else asked[d]
            column = jnp.broadcast_to(lists[:, dz * 4 + d : dz * 4 + d + 1], (SLOT, FD))
            chosen = jnp.where(slot_lane == column, 1.0, 0.0).astype(BF16)
            got = nn(chosen, block).astype(BF16)
            if d == 0:
                rows[dz * 4] = got
            else:
                pick[dz, d] = got
                copy = remote(pick.at[dz, d], rows.at[dz * 4 + d], row_sem, (dz, d), x_of[d])
                copy.start()
                sends.append(copy)
        return sends

    sends = {0: serve(0)}

    mine.wait()
    for copy in msgs:
        copy.wait()
    lam = [jnp.sum(msg_in[j, pl.ds(DV, 16), :].astype(F32), axis=0, keepdims=True) for j in range(8)]
    grow = [jnp.exp(v) for v in lam]
    prefix, reach = [jnp.zeros((DV, FD), F32)], [jnp.zeros((1, FD), F32)]
    for j in range(8):
        prefix.append(grow[j] * prefix[-1] + msg_in[j, pl.ds(0, DV), :].astype(F32))
        reach.append(reach[-1] + lam[j])
    y_out[pl.ds(0, DV), :] = prefix[8]
    y_out[pl.ds(DV, 8), :] = jnp.broadcast_to(reach[8], (8, FD))
    y_copies = [remote(y_out, y_in.at[(4 - d) % 4], y_sem, (d,), y_of[d]) for d in range(1, 4)]
    for copy in y_copies:
        copy.start()

    up[0].wait()
    far_up.start()
    dn[0].wait()
    far_dn.start()

    for copy in y_copies:
        copy.wait()
    carry = jnp.zeros((DV, FD), F32)
    for d in range(1, 4):
        step = jnp.exp(y_in[d, pl.ds(DV, 1), :]) * carry + y_in[d, pl.ds(0, DV), :]
        carry = jnp.where(d >= 4 - y, step, carry)
    for j in range(8):
        ent_out[j] = (prefix[j] + jnp.exp(reach[j]) * carry).astype(BF16)
    own_entry = pltpu.make_async_copy(ent_out.at[i], ent.at[i], load_sem.at[8])
    own_entry.start()
    entries = [remote(ent_out.at[(i + d) % 8], ent.at[i], ent_sem, (d,), row_of[d]) for d in range(1, 8)]
    for copy in entries:
        copy.start()

    up[1].wait()
    sends[1] = serve(1)
    dn[1].wait()
    sends[3] = serve(3)

    loads[6].wait()
    own_entry.wait()
    for copy in entries:
        copy.wait()
    halves = []
    for h in range(H):
        carried = nt(ent[h], q_s[:, h * DK : (h + 1) * DK]) * (jnp.exp(cum[h : h + 1, :]) * scale)
        attended = inside[h] + carried
        halves.append(attended * lax.rsqrt(jnp.mean(attended * attended, axis=0, keepdims=True) + 1e-05))
    context = jnp.concatenate(
        [jnp.concatenate(halves[2 * c : 2 * c + 2], axis=0).T.astype(BF16) for c in range(E // FD)], axis=1
    )
    predicted = [nn(context, wp[k]).astype(BF16) for k in range(K)]

    @pl.when(has_prev)
    def _():
        fut_copy.wait_send()

    @pl.when(has_next)
    def _():
        fut_copy.wait_recv()
        halo_copy.wait_send()

    @pl.when(jnp.logical_not(has_next))
    def _():
        fut[...] = jnp.zeros_like(fut)

    inv_width = 1.0 / math.sqrt(E)
    valid_lane = jnp.where(lane[0:1, :] + m * FD < length, inv_width, 0.0)
    later = iota((16, FD), 0) + FD
    later_lane = iota((16, FD), 1)
    for k in range(K):
        here = jnp.where(sub == lane + (k + 1), nt(grid[0], predicted[k]), 0.0)
        ahead = jnp.where(later == later_lane + (k + 1), nt(fut[...], predicted[k]), 0.0)
        positive = jnp.sum(here, axis=0, keepdims=True) + jnp.sum(ahead, axis=0, keepdims=True)
        out_ref[0, k, 0:1, :] = positive * valid_lane

    negative = [[jnp.zeros((1, FD), F32) for _ in range(NNEG)] for _ in range(K)]

    def score(dz):
        start = 1 if dz == 0 else 0
        for d in range(start, 4):
            n = dz * 4 + d
            block = rows[n]
            found = [slot_rows + n * SLOT == spot[j] for j in range(NNEG)]
            for k in range(K):
                scores = nt(block, predicted[k])
                for j in range(NNEG):
                    negative[k][j] += jnp.sum(jnp.where(found[j], scores, 0.0), axis=0, keepdims=True)

    far_up.wait()
    far_dn.wait()
    sends[2] = serve(2)
    for dz in (0, 1, 3, 2):
        for copy in sends[dz]:
            copy.wait()
        score(dz)
    for k in range(K):
        for j in range(NNEG):
            out_ref[0, k, 1 + j : 2 + j, :] = negative[k][j] * valid_lane


def shards(raw, w_conv, w_query, w_key, w_pred, log_decay, lengths, neg_offset, neg_frame):
    aux = jnp.concatenate(
        [neg_offset[0].T, neg_frame[0].T, jnp.broadcast_to(lengths[0], (2, FD))], axis=0
    )
    hbm = pl.BlockSpec(memory_space=pl.ANY)
    dma = pltpu.SemaphoreType.DMA
    return pl.pallas_call(
        kernel,
        out_shape=jax.ShapeDtypeStruct((1, K, 1 + NNEG, FD), F32),
        in_specs=[hbm] * 7,
        out_specs=pl.BlockSpec(memory_space=pltpu.VMEM),
        scratch_shapes=[
            pltpu.VMEM((FD, FRAME_W), BF16),
            pltpu.VMEM((2 * FRAME_W, E), BF16),
            pltpu.VMEM((E, DA), BF16),
            pltpu.VMEM((E, DA), BF16),
            pltpu.VMEM((K, E, E), BF16),
            pltpu.VMEM((H, FD), F32),
            pltpu.VMEM((8, FD), I32),
            pltpu.VMEM((16, FRAME_W), BF16),
            pltpu.VMEM((16, E), BF16),
            pltpu.VMEM((SLOT, FD), I32),
            pltpu.VMEM((4, SLOT, FD), I32),
            pltpu.VMEM((4, FD, E), BF16),
            pltpu.VMEM((4, 4, SLOT, E), BF16),
            pltpu.VMEM((16, SLOT, E), BF16),
            pltpu.VMEM((H, MSG, FD), BF16),
            pltpu.VMEM((H, MSG, FD), BF16),
            pltpu.VMEM((YMSG, FD), F32),
            pltpu.VMEM((4, YMSG, FD), F32),
            pltpu.VMEM((H, DV, FD), BF16),
            pltpu.VMEM((H, DV, FD), BF16),
            pltpu.VMEM((FD, DA), BF16),
            pltpu.VMEM((H, DV, FD), F32),
            dma((9,)),
            dma((2,)),
            dma((2,)),
            dma((2, 4)),
            dma((2, 2, 2)),
            dma((2, 2)),
            dma((2, 4, 4)),
            dma((2, 8)),
            dma((2, 4)),
            dma((2, 8)),
        ],
        compiler_params=pltpu.CompilerParams(collective_id=0, has_side_effects=True),
    )(raw, w_conv, w_query, w_key, w_pred, log_decay, aux)


def solution(mesh):
    placed = (
        P("batch", "tm", None),
        P(),
        P(),
        P(),
        P(),
        P("batch", None, "tm"),
        P("batch"),
        P("batch", "tm", None),
        P("batch", "tm", None),
    )
    return jax.shard_map(
        shards, mesh=mesh, in_specs=placed, out_specs=P("batch", None, None, "tm"), check_vma=False
    )
```

time: 262 us -> 55 us (0.21)
  waiting for transfers between devices: 114 us -> 0 us
  local copies, waits for them, and re-layouts: 66.4 us -> 2.04 us
  Pallas kernels: 0 us -> 51.5 us
  blocking collectives: 44 us -> 0 us
  between operations: 14.3 us -> 0.67 us
  matrix products: 7.05 us -> 0 us
  starting transfers between devices: 7.03 us -> 0 us
  other arithmetic: 6.05 us -> 0.66 us
    all_gather x2 -> x0, waiting for transfers between devices: 113 us -> none  [the longest x1 66.6 us: carried_in(): pieces = jax.tree.map(lambda part: lax.all_gather(part, axis), value)]
    pallas_call x0 -> x1, Pallas kernels: none -> 51.5 us  [shards(): pl.pallas_call(kernel, out_shape=jax.ShapeDtypeStruct((1, K, 1 + NNEG, FD...]
    all_gather x1 -> x0, blocking collectives: 44 us -> none  [carried_in(): pieces = jax.tree.map(lambda part: lax.all_gather(part, axis), value)]
    dynamic_slice x62 -> x0, local copies, waits for them, and re-layouts: 36.4 us -> none  [turn(): longer = join(subtotal, jax.tree.map(lambda part: part[position], pieces))]
    mul x31 -> x0, local copies, waits for them, and re-layouts: 21.4 us -> none  [combine(): later_pair[0][:, None, None] * earlier_pair[1] + later_pair[1]]
    dot_general x11 -> x0, matrix products: 7.05 us -> none  [the longest x1 1.44 us: shards(): jnp.dot(signal, w_conv[width_in:], preferred_element_type=jnp.float32)]
    ppermute x2 -> x0, starting transfers between devices: 6.99 us -> none  [passed_along(): lax.ppermute(value, axis, [(source, source + steps) for source in range(l...]
    select_n x32 -> x0, other arithmetic: 4.21 us -> none  [the longest x31 4.19 us: turn(): jnp.where(position < mine, new, old)]
  transfers between devices with their start and end apart: 4 -> 0, of which waited for: 3 -> 0; matrix products, arithmetic and copies ran while one was open for 29% -> 0% of each run, Pallas kernels for 0% -> 0%
where the time goes in v1:
time: 55 us; the launch traced here: 54.9 us
  Pallas kernels  51.5 us (94%)
  local copies, waits for them, and re-layouts  2.04 us (4%)
  between operations  0.67 us (1%)
  other arithmetic  0.66 us (1%)
    pallas_call x1, Pallas kernels, shards(): pl.pallas_call(kernel, out_shape=jax.ShapeDtypeStruct((1, K, 1 + NNEG, FD...  51.5 us
    unnamed x1, local copies, waits for them, and re-layouts  1.26 us

profile of v1, /device:TPU:1, one launch (start us, length us, event | category | flops | bytes accessed | tf_op | source)
XLA Modules:
  0.0 54.9 jit_solution(13722164539082781844)
XLA Ops:
  0.7 0.1 pad.2.clone
  0.7 0.7 %copy_bitcast_fusion = (s32[3,128]{1,0:T(4,128)S(1)}, s32[3,128]{1,0:T(4,128)S(1)}) fusion(s32[1,128,3]{1,0,2:T(1,128)} %param.17, s32[1,128,3]{1,0,2:T(1,128)} %param.16), kind=kLoop, calls=%fused_computation.1 | loop fusion | bytes 6144 | tf_op jit(solution)/shard_map/transpose | solution.py:330
  1.4 0.7 %add_add_fusion.aux_hbm = s32[8,128]{1,0:T(8,128)} fusion(s32[3,128]{1,0:T(4,128)S(1)} %get-tuple-element.5, s32[3,128]{1,0:T(4,128)S(1)} %get-tuple-element.6, s32[8]{0:T(128)S(1)} %pad.2.clone), kind=kLoop, calls=%fused_computation | loop fusion | flops 2048 | bytes 7200 | tf_op jit(solution)/shard_map/concatenate | solution.py:329
  2.1 51.5 %shard_map.91 = f32[1,2,4,128]{3,2,1,0:T(4,128)} custom-call(bf16[1,128,640]{2,1,0:T(8,128)(2,1)} %raw_hbm.1, bf16[1280,512]{1,0:T(8,128)(2,1)} %wc_hbm.1, bf16[512,1024]{1,0:T(8,128)(2,1)} %wq_hbm.1, bf16[512,1024]{1,0:T(8,128)(2,1)} %wk_hbm.1, bf16[2,512,512]{2,1,0:T(8,128)(2,1)} %wp_hbm.1, f32[1,8,128]{2,1,0:T(8,128)} %ld_hbm.1, s32[8,128]{1,0:T(8,128)} %add_add_fusion.aux_hbm), custom_call_target="tpu_custom_call" | custom-call | tf_op jit(solution)/shard_map/pallas_call | solution.py:334
  53.6 1.3 %copy.16 = f32[1,2,4,128]{3,2,1,0:T(4,128)} copy(f32[1,2,4,128]{3,2,1,0:T(4,128)} %shard_map.91) | data formatting | bytes 8192
  (1 shorter events, 0.0 us)

commit v2 on v1

v2 whole, which is shorter than its diff:
```python
import functools
import math

import jax
import jax.numpy as jnp
from jax import lax
from jax.experimental import pallas as pl
from jax.experimental.pallas import tpu as pltpu
from jax.sharding import PartitionSpec as P

MESH = pl.DeviceIdType.MESH
F32, BF16, I32 = jnp.float32, jnp.bfloat16, jnp.int32
FD, E, DA, H, FRAME_W, K, NNEG = 128, 512, 1024, 8, 640, 2, 3
DK, DV = DA // H, E // H
SLOT = 48
CHUNK = FD // 4
MSG = DV + 16
YMSG = DV + 8


def nt(a, b):
    return lax.dot_general(a, b, (((1,), (1,)), ((), ())), preferred_element_type=F32)


def nn(a, b):
    return jnp.dot(a, b, preferred_element_type=F32)


def iota(shape, axis):
    return lax.broadcasted_iota(I32, shape, axis)


def kernel(
    raw_hbm, wc_hbm, wq_hbm, wk_hbm, wp_hbm, ld_hbm, off_hbm, frm_hbm, len_ref, out_ref,
    raw, wc, wq, wk, wp, ld, off, frm, halo, fut, want, asked, grid, pick, rows,
    st_out, st_in, msg_out, msg_in, y_out, y_in, ent_out, ent_in, ent_pair, ent, q_s, inside,
    load_sem, halo_sem, fut_sem, ask_sem, near_sem, far_sem, row_sem, pair_sem, msg_sem, y_sem, ent_sem,
):
    b, m = lax.axis_index("batch"), lax.axis_index("tm")
    zh, x = b // 4, b % 4
    y, zl, c = m // 8, (m // 2) % 4, m % 2

    def remote(src, dst, sems, index, dev):
        return pltpu.make_async_remote_copy(
            src_ref=src, dst_ref=dst, send_sem=sems.at[(0, *index)], recv_sem=sems.at[(1, *index)],
            device_id=dev, device_id_type=MESH,
        )

    loads = [
        pltpu.make_async_copy(src, dst, load_sem.at[n])
        for n, (src, dst) in enumerate(
            [(raw_hbm.at[0], raw), (wc_hbm, wc), (off_hbm, off), (frm_hbm, frm), (ld_hbm.at[0], ld),
             (wk_hbm, wk), (wq_hbm, wq), (wp_hbm, wp)]
        )
    ]
    loads[0].start()
    loads[1].start()

    z_up, z_dn = (((zh + 1) % 4) * 4 + x, m), (((zh + 3) % 4) * 4 + x, m)
    x_of = [(zh * 4 + (x + d) % 4, m) for d in range(4)]
    pair = (b, m + 1 - 2 * c)
    row_of = [(b, y * 8 + ((zl + d) % 4) * 2 + c) for d in range(4)]
    y_of = [(b, ((y + d) % 4) * 8 + zl * 2 + c) for d in range(4)]
    nxt, prv = (b, jnp.minimum(m + 1, 31)), (b, jnp.maximum(m - 1, 0))
    has_next, has_prev = m < 31, m > 0
    edge_next = jnp.logical_and(c == 1, has_next)
    edge_prev = jnp.logical_and(c == 0, has_prev)

    barrier = pltpu.get_barrier_semaphore()
    for dev in [z_up, z_dn] + x_of[1:] + y_of[1:] + row_of[1:] + [pair]:
        pl.semaphore_signal(barrier, inc=1, device_id=dev, device_id_type=MESH)

    @pl.when(edge_next)
    def _():
        pl.semaphore_signal(barrier, inc=1, device_id=nxt, device_id_type=MESH)

    @pl.when(edge_prev)
    def _():
        pl.semaphore_signal(barrier, inc=1, device_id=prv, device_id_type=MESH)

    for load in loads[2:]:
        load.start()

    lane = iota((FD, FD), 1)
    sub = iota((FD, FD), 0)
    length = len_ref[0]
    valid_rows = jnp.where(sub + m * FD < length, 1.0, 0.0)
    valid_rows = jnp.concatenate([valid_rows] * 4, axis=1)

    def encode(hidden, valid):
        u = jax.nn.gelu(hidden)
        return (u * lax.rsqrt(jnp.mean(u * u, axis=-1, keepdims=True) + 1e-05) * valid).astype(BF16)

    loads[0].wait()
    loads[1].wait()
    before = pltpu.roll(nn(raw[...], wc[:FRAME_W, :]), 1, 0)
    now = nn(raw[...], wc[FRAME_W:, :])
    enc = encode(now + before, valid_rows)
    grid[0] = enc

    def part(n):
        return pl.ds(n * CHUNK, CHUNK)

    up_order, dn_order = (3, 2, 1, 0), (1, 0, 3, 2)
    up = [remote(grid.at[0, part(n), :], grid.at[1, part(n), :], near_sem, (0, n), z_up) for n in range(4)]
    dn = [remote(grid.at[0, part(n), :], grid.at[3, part(n), :], near_sem, (1, n), z_dn) for n in range(4)]
    far_up = [remote(grid.at[1, part(n), :], grid.at[2, part(n), :], far_sem, (0, n % 2), z_up) for n in (3, 2)]
    far_dn = [remote(grid.at[3, part(n), :], grid.at[2, part(n), :], far_sem, (1, n % 2), z_dn) for n in (1, 0)]
    halo_copy = remote(raw.at[pl.ds(FD - 16, 16), :], halo, halo_sem, (), nxt)
    fut_copy = remote(grid.at[0, pl.ds(0, 16), :], fut, fut_sem, (), prv)
    asks = [remote(want, asked.at[d], ask_sem, (d,), x_of[(4 - d) % 4]) for d in range(1, 4)]

    edges = jnp.where(c == 1, jnp.where(has_next, 1, 0), jnp.where(has_prev, 1, 0))
    pl.semaphore_wait(barrier, 12 + edges)

    @pl.when(has_next)
    def _():
        halo_copy.start()

    up[3].start()
    dn[1].start()

    loads[2].wait()
    loads[3].wait()
    rel_j, frame_j = [], []
    for j in range(NNEG):
        group = (b + off[j] + 1) & 15
        rel_j.append((((zh - (group >> 2)) & 3) << 2) | ((x - (group & 3)) & 3))
        frame_j.append(frm[j])
    rel_rows = iota((16, FD), 0)
    hit = [jnp.where(rel_rows == rel_j[j], 1, 0) for j in range(NNEG)]
    named = hit[0] + hit[1] + hit[2]
    frame_of = hit[0] * frame_j[0] + hit[1] * frame_j[1] + hit[2] * frame_j[2]
    upto = jnp.where(sub <= lane, 1.0, 0.0).astype(BF16)
    rank = nn(named.astype(F32).astype(BF16), upto).astype(I32) - 1
    spot = [jnp.sum(hit[j] * (rel_rows * SLOT + rank), axis=0, keepdims=True) for j in range(NNEG)]
    code = jnp.where(named > 0, rank, -1)
    slot_rows = iota((SLOT, FD), 0)
    slot_lane = iota((SLOT, FD), 1)
    wanted = jnp.zeros((SLOT, FD), I32)
    for r in range(1, 16):
        column = jnp.sum(
            jnp.where(slot_rows == code[r : r + 1, :], frame_of[r : r + 1, :].astype(F32), 0.0), axis=1, keepdims=True
        )
        wanted = jnp.where(slot_lane == r, column.astype(I32), wanted)
    want[...] = wanted
    for copy in asks:
        copy.start()

    loads[4].wait()
    cum = ld[...]
    lane8 = iota((H, FD), 1)
    for shift in (1, 2, 4, 8, 16, 32, 64):
        cum = cum + jnp.where(lane8 >= shift, pltpu.roll(cum, shift, 1), 0.0)
    cum_col = jnp.concatenate([cum, jnp.zeros((FD - H, FD), F32)], axis=0).T
    total = jnp.sum(jnp.where(lane8 == FD - 1, cum, 0.0), axis=1, keepdims=True)
    total_row = jnp.broadcast_to(total, (H, FD))

    @pl.when(has_prev)
    def _():
        halo_copy.wait_recv()

    @pl.when(jnp.logical_not(has_prev))
    def _():
        halo[...] = jnp.zeros_like(halo)

    edge = nn(halo[...], wc[:FRAME_W, :])
    first = iota((16, E), 0) == 0
    top = encode(
        now[:16, :] + jnp.where(first, jnp.broadcast_to(edge[15:16, :], (16, E)), before[:16, :]), valid_rows[:16, :]
    )
    grid[0, pl.ds(0, 16), :] = top
    enc = jnp.concatenate([top, enc[16:, :]], axis=0)
    up[2].start()
    dn[0].start()

    @pl.when(has_prev)
    def _():
        fut_copy.start()

    loads[5].wait()
    enc_t = [enc[:, n * FD : (n + 1) * FD].T for n in range(E // FD)]
    value_t = [enc_t[h // 2][(h % 2) * DV : (h % 2 + 1) * DV, :] for h in range(H)]
    keys = nn(enc, wk[...]).astype(BF16)
    for h in range(H):
        key = keys[:, h * DK : (h + 1) * DK]
        to_end = jnp.exp(total_row[h : h + 1, :] - jnp.broadcast_to(cum_col[:, h : h + 1], (FD, FD)))
        weighted = (key.astype(F32) * to_end).astype(BF16)
        st_out[h, pl.ds(0, DV), :] = nn(value_t[h], weighted)
        st_out[h, pl.ds(DV, 8), :] = jnp.broadcast_to(total_row[h : h + 1, :], (8, FD))
    pair_copy = remote(st_out.at[pl.ds(4 - 4 * c, 4)], st_in, pair_sem, (0,), pair)
    pair_copy.start()

    loads[6].wait()
    queries = nn(enc, wq[...]).astype(BF16)
    q_s[...] = queries

    def core_states(n):
        own, other = st_out[4 * c + n], st_in[n]
        return jnp.where(c == 0, own, other), jnp.where(c == 0, other, own)

    pair_copy.wait()
    rows16 = iota((16, FD), 0)
    for n in range(4):
        early, late = core_states(n)
        joined = jnp.exp(late[DV : DV + 1, :]) * early[:DV, :] + late[:DV, :]
        whole = early[DV : DV + 1, :] + late[DV : DV + 1, :]
        hi = whole.astype(BF16).astype(F32)
        mid = (whole - hi).astype(BF16).astype(F32)
        lo = whole - hi - mid
        pieces = jnp.where(rows16 == 0, hi, jnp.where(rows16 == 1, mid, jnp.where(rows16 == 2, lo, 0.0)))
        msg_out[n, pl.ds(0, DV), :] = joined.astype(BF16)
        msg_out[n, pl.ds(DV, 16), :] = pieces.astype(BF16)
    msgs = [remote(msg_out.at[(zl + d) % 4], msg_in.at[zl], msg_sem, (d,), row_of[d]) for d in range(1, 4)]
    for copy in msgs:
        copy.start()
    msg_in[zl] = msg_out[zl]
    for n in range(2, 4):
        up[up_order[n]].start()
        dn[dn_order[n]].start()

    scale = 1.0 / math.sqrt(DK)
    for h in range(H):
        key = keys[:, h * DK : (h + 1) * DK]
        query = queries[:, h * DK : (h + 1) * DK]
        gap = cum[h : h + 1, :] - jnp.broadcast_to(cum_col[:, h : h + 1], (FD, FD))
        weight = jnp.where(sub <= lane, jnp.exp(jnp.minimum(gap, 0.0)), 0.0)
        probs_t = (nt(key, query) * weight * scale).astype(BF16)
        inside[h] = nn(value_t[h], probs_t)

    for copy in asks:
        copy.wait()

    def serve(dz):
        block = grid[dz]
        sends = []
        for d in range(4):
            if dz == 0 and d == 0:
                continue
            lists = want[...] if d == 0 else asked[d]
            column = jnp.broadcast_to(lists[:, dz * 4 + d : dz * 4 + d + 1], (SLOT, FD))
            chosen = jnp.where(slot_lane == column, 1.0, 0.0).astype(BF16)
            got = nn(chosen, block).astype(BF16)
            if d == 0:
                rows[dz * 4] = got
            else:
                pick[dz, d] = got
                copy = remote(pick.at[dz, d], rows.at[dz * 4 + d], row_sem, (dz, d), x_of[d])
                copy.start()
                sends.append(copy)
        return sends

    sends = {0: serve(0)}

    up[3].wait()
    far_up[0].start()
    dn[1].wait()
    far_dn[0].start()

    for copy in msgs:
        copy.wait()
    lam = [jnp.sum(msg_in[n, pl.ds(DV, 16), :].astype(F32), axis=0, keepdims=True) for n in range(4)]
    prefix, reach = [jnp.zeros((DV, FD), F32)], [jnp.zeros((1, FD), F32)]
    for n in range(4):
        prefix.append(jnp.exp(lam[n]) * prefix[-1] + msg_in[n, pl.ds(0, DV), :].astype(F32))
        reach.append(reach[-1] + lam[n])
    y_out[pl.ds(0, DV), :] = prefix[4]
    y_out[pl.ds(DV, 8), :] = jnp.broadcast_to(reach[4], (8, FD))
    y_copies = [remote(y_out, y_in.at[(4 - d) % 4], y_sem, (d,), y_of[d]) for d in range(1, 4)]
    for copy in y_copies:
        copy.start()

    up[2].wait()
    far_up[1].start()
    dn[0].wait()
    far_dn[1].start()

    for copy in y_copies:
        copy.wait()
    carry = jnp.zeros((DV, FD), F32)
    for d in range(1, 4):
        step = jnp.exp(y_in[d, pl.ds(DV, 1), :]) * carry + y_in[d, pl.ds(0, DV), :]
        carry = jnp.where(d >= 4 - y, step, carry)
    for n in range(4):
        ent_out[n] = (prefix[n] + jnp.exp(reach[n]) * carry).astype(BF16)
    entries = [remote(ent_out.at[(zl + d) % 4], ent_in.at[zl], ent_sem, (d,), row_of[d]) for d in range(1, 4)]
    for copy in entries:
        copy.start()
    ent_in[zl] = ent_out[zl]

    for n in range(2):
        up[n].wait()
    sends[1] = serve(1)
    for n in range(2, 4):
        dn[n].wait()
    sends[3] = serve(3)

    for copy in entries:
        copy.wait()
    for n in range(4):
        early, _ = core_states(n)
        at_first = ent_in[n].astype(F32)
        at_second = jnp.exp(early[DV : DV + 1, :]) * at_first + early[:DV, :]
        ent[4 * c + n] = jnp.where(c == 0, at_first, at_second).astype(BF16)
        ent_pair[n] = jnp.where(c == 0, at_second, at_first).astype(BF16)
    back_copy = remote(ent_pair, ent.at[pl.ds(4 * c, 4)], pair_sem, (1,), pair)
    back_copy.start()
    loads[7].wait()
    back_copy.wait()
    halves = []
    for h in range(H):
        carried = nt(ent[h], q_s[:, h * DK : (h + 1) * DK]) * (jnp.exp(cum[h : h + 1, :]) * scale)
        attended = inside[h] + carried
        halves.append(attended * lax.rsqrt(jnp.mean(attended * attended, axis=0, keepdims=True) + 1e-05))
    context = jnp.concatenate(
        [jnp.concatenate(halves[2 * n : 2 * n + 2], axis=0).T.astype(BF16) for n in range(E // FD)], axis=1
    )
    predicted = [nn(context, wp[k]).astype(BF16) for k in range(K)]

    @pl.when(has_prev)
    def _():
        fut_copy.wait_send()

    @pl.when(has_next)
    def _():
        fut_copy.wait_recv()
        halo_copy.wait_send()

    @pl.when(jnp.logical_not(has_next))
    def _():
        fut[...] = jnp.zeros_like(fut)

    for copy in far_up + far_dn:
        copy.wait()
    sends[2] = serve(2)

    inv_width = 1.0 / math.sqrt(E)
    valid_lane = jnp.where(lane[0:1, :] + m * FD < length, inv_width, 0.0)
    later = iota((16, FD), 0) + FD
    later_lane = iota((16, FD), 1)
    for k in range(K):
        here = jnp.where(sub == lane + (k + 1), nt(grid[0], predicted[k]), 0.0)
        ahead = jnp.where(later == later_lane + (k + 1), nt(fut[...], predicted[k]), 0.0)
        positive = jnp.sum(here, axis=0, keepdims=True) + jnp.sum(ahead, axis=0, keepdims=True)
        out_ref[0, k, 0:1, :] = positive * valid_lane

    negative = [[jnp.zeros((1, FD), F32) for _ in range(NNEG)] for _ in range(K)]

    def score(dz):
        start = 1 if dz == 0 else 0
        for d in range(start, 4):
            n = dz * 4 + d
            block = rows[n]
            found = [slot_rows + n * SLOT == spot[j] for j in range(NNEG)]
            for k in range(K):
                scores = nt(block, predicted[k])
                for j in range(NNEG):
                    negative[k][j] += jnp.sum(jnp.where(found[j], scores, 0.0), axis=0, keepdims=True)

    for dz in (0, 1, 3, 2):
        for copy in sends[dz]:
            copy.wait()
        score(dz)
    for k in range(K):
        for j in range(NNEG):
            out_ref[0, k, 1 + j : 2 + j, :] = negative[k][j] * valid_lane


def shards(raw, w_conv, w_query, w_key, w_pred, log_decay, lengths, neg_offset, neg_frame):
    hbm = pl.BlockSpec(memory_space=pl.ANY)
    dma = pltpu.SemaphoreType.DMA
    return pl.pallas_call(
        kernel,
        out_shape=jax.ShapeDtypeStruct((1, K, 1 + NNEG, FD), F32),
        in_specs=[hbm] * 8 + [pl.BlockSpec(memory_space=pltpu.SMEM)],
        out_specs=pl.BlockSpec(memory_space=pltpu.VMEM),
        scratch_shapes=[
            pltpu.VMEM((FD, FRAME_W), BF16),
            pltpu.VMEM((2 * FRAME_W, E), BF16),
            pltpu.VMEM((E, DA), BF16),
            pltpu.VMEM((E, DA), BF16),
            pltpu.VMEM((K, E, E), BF16),
            pltpu.VMEM((H, FD), F32),
            pltpu.VMEM((NNEG, 1, FD), I32),
            pltpu.VMEM((NNEG, 1, FD), I32),
            pltpu.VMEM((16, FRAME_W), BF16),
            pltpu.VMEM((16, E), BF16),
            pltpu.VMEM((SLOT, FD), I32),
            pltpu.VMEM((4, SLOT, FD), I32),
            pltpu.VMEM((4, FD, E), BF16),
            pltpu.VMEM((4, 4, SLOT, E), BF16),
            pltpu.VMEM((16, SLOT, E), BF16),
            pltpu.VMEM((H, DV + 8, FD), F32),
            pltpu.VMEM((4, DV + 8, FD), F32),
            pltpu.VMEM((4, MSG, FD), BF16),
            pltpu.VMEM((4, MSG, FD), BF16),
            pltpu.VMEM((YMSG, FD), F32),
            pltpu.VMEM((4, YMSG, FD), F32),
            pltpu.VMEM((4, DV, FD), BF16),
            pltpu.VMEM((4, DV, FD), BF16),
            pltpu.VMEM((4, DV, FD), BF16),
            pltpu.VMEM((H, DV, FD), BF16),
            pltpu.VMEM((FD, DA), BF16),
            pltpu.VMEM((H, DV, FD), F32),
            dma((8,)),
            dma((2,)),
            dma((2,)),
            dma((2, 4)),
            dma((2, 2, 4)),
            dma((2, 2, 2)),
            dma((2, 4, 4)),
            dma((2, 2)),
            dma((2, 4)),
            dma((2, 4)),
            dma((2, 4)),
        ],
        compiler_params=pltpu.CompilerParams(collective_id=0, has_side_effects=True),
    )(
        raw, w_conv, w_query, w_key, w_pred, log_decay,
        jnp.transpose(neg_offset, (2, 0, 1)), jnp.transpose(neg_frame, (2, 0, 1)), lengths,
    )


def solution(mesh):
    placed = (
        P("batch", "tm", None),
        P(),
        P(),
        P(),
        P(),
        P("batch", None, "tm"),
        P("batch"),
        P("batch", "tm", None),
        P("batch", "tm", None),
    )
    return jax.shard_map(
        shards, mesh=mesh, in_specs=placed, out_specs=P("batch", None, None, "tm"), check_vma=False
    )
```

time: 55 us -> 49.2 us (0.89)
  Pallas kernels: 51.5 us -> 47.1 us
  local copies, waits for them, and re-layouts: 2.04 us -> 1.28 us
  other arithmetic: 0.66 us -> 0 us
    pallas_call x1, Pallas kernels: 51.5 us -> 47.1 us  [shards(): pl.pallas_call(kernel, out_shape=jax.ShapeDtypeStruct((1, K, 1 + NNEG, FD...]
    transpose x1 -> x0, local copies, waits for them, and re-layouts: 0.7 us -> none  [shards(): neg_frame[0]]
    concatenate x1 -> x0, other arithmetic: 0.66 us -> none  [shards(): jnp.concatenate([neg_offset[0].T, neg_frame[0].T, jnp.broadcast_to(length...]
where the time goes in v2:
time: 49.2 us; the launch traced here: 49 us
  Pallas kernels  47.1 us (96%)
  local copies, waits for them, and re-layouts  1.28 us (3%)
  between operations  0.66 us (1%)
    pallas_call x1, Pallas kernels, shards(): pl.pallas_call(kernel, out_shape=jax.ShapeDtypeStruct((1, K, 1 + NNEG, FD...  47.1 us
    unnamed x1, local copies, waits for them, and re-layouts  1.28 us

profile of v2, /device:TPU:1, one launch (start us, length us, event | category | flops | bytes accessed | tf_op | source)
XLA Modules:
  0.0 49.0 jit_solution(10244530654566013264)
XLA Ops:
  0.7 47.1 %shard_map.91 = f32[1,2,4,128]{3,2,1,0:T(4,128)} custom-call(bf16[1,128,640]{2,1,0:T(8,128)(2,1)} %raw_hbm.1, bf16[1280,512]{1,0:T(8,128)(2,1)} %wc_hbm.1, bf16[512,1024]{1,0:T(8,128)(2,1)} %wq_hbm.1, bf16[512,1024]{1,0:T(8,128)(2,1)} %wk_hbm.1, bf16[2,512,512]{2,1,0:T(8,128)(2,1)} %wp_hbm.1, f32[1,8,128]{2,1,0:T(8,128)} %ld_hbm.1, s32[3,1,128]{2,1,0:T(1,128)} %bitcast.2, ...), custom_call_target="tpu_custom_call" | custom-call | tf_op jit(solution)/shard_map/pallas_call | solution.py:372
  47.8 1.3 %copy.12 = f32[1,2,4,128]{3,2,1,0:T(4,128)} copy(f32[1,2,4,128]{3,2,1,0:T(4,128)} %shard_map.91) | data formatting | bytes 8192

commit v3 on v2

--- a/solution.py
+++ b/solution.py
@@ -12,7 +12,7 @@
 F32, BF16, I32 = jnp.float32, jnp.bfloat16, jnp.int32
 FD, E, DA, H, FRAME_W, K, NNEG = 128, 512, 1024, 8, 640, 2, 3
 DK, DV = DA // H, E // H
-SLOT = 48
+SLOT, PAD = 40, 48
 CHUNK = FD // 4
 MSG = DV + 16
 YMSG = DV + 8
@@ -33,16 +33,16 @@
 def kernel(
     raw_hbm, wc_hbm, wq_hbm, wk_hbm, wp_hbm, ld_hbm, off_hbm, frm_hbm, len_ref, out_ref,
     raw, wc, wq, wk, wp, ld, off, frm, halo, fut, want, asked, grid, pick, rows,
-    st_out, st_in, msg_out, msg_in, y_out, y_in, ent_out, ent_in, ent_pair, ent, q_s, inside,
+    chosen, st_out, st_in, msg_out, msg_in, y_out, y_in, ent_out, ent_in, ent_pair, ent, q_s, inside,
     load_sem, halo_sem, fut_sem, ask_sem, near_sem, far_sem, row_sem, pair_sem, msg_sem, y_sem, ent_sem,
 ):
     b, m = lax.axis_index("batch"), lax.axis_index("tm")
     zh, x = b // 4, b % 4
     y, zl, c = m // 8, (m // 2) % 4, m % 2
 
-    def remote(src, dst, sems, index, dev):
+    def remote(src, dst, sems, out, back, dev):
         return pltpu.make_async_remote_copy(
-            src_ref=src, dst_ref=dst, send_sem=sems.at[(0, *index)], recv_sem=sems.at[(1, *index)],
+            src_ref=src, dst_ref=dst, send_sem=sems.at[out], recv_sem=sems.at[back],
             device_id=dev, device_id_type=MESH,
         )
 
@@ -101,14 +101,22 @@
     def part(n):
         return pl.ds(n * CHUNK, CHUNK)
 
-    up_order, dn_order = (3, 2, 1, 0), (1, 0, 3, 2)
-    up = [remote(grid.at[0, part(n), :], grid.at[1, part(n), :], near_sem, (0, n), z_up) for n in range(4)]
-    dn = [remote(grid.at[0, part(n), :], grid.at[3, part(n), :], near_sem, (1, n), z_dn) for n in range(4)]
-    far_up = [remote(grid.at[1, part(n), :], grid.at[2, part(n), :], far_sem, (0, n % 2), z_up) for n in (3, 2)]
-    far_dn = [remote(grid.at[3, part(n), :], grid.at[2, part(n), :], far_sem, (1, n % 2), z_dn) for n in (1, 0)]
-    halo_copy = remote(raw.at[pl.ds(FD - 16, 16), :], halo, halo_sem, (), nxt)
-    fut_copy = remote(grid.at[0, pl.ds(0, 16), :], fut, fut_sem, (), prv)
-    asks = [remote(want, asked.at[d], ask_sem, (d,), x_of[(4 - d) % 4]) for d in range(1, 4)]
+    low, high = pl.ds(0, 2 * CHUNK), pl.ds(2 * CHUNK, 2 * CHUNK)
+    up = [remote(grid.at[0, part(n), :], grid.at[1, part(n), :], near_sem, 0, 2 + max(n - 1, 0), z_up) for n in range(4)]
+    dn = [remote(grid.at[0, part(n), :], grid.at[3, part(n), :], near_sem, 1, 5 + min(n, 2), z_dn) for n in range(4)]
+    up_all, dn_all = remote(grid.at[0], grid.at[1], near_sem, 0, 2, z_up), remote(grid.at[0], grid.at[3], near_sem, 1, 7, z_dn)
+    up_rest = remote(grid.at[0, low, :], grid.at[1, low, :], near_sem, 0, 2, z_up)
+    dn_rest = remote(grid.at[0, high, :], grid.at[3, high, :], near_sem, 1, 7, z_dn)
+    far_up = [remote(grid.at[1, part(n), :], grid.at[2, part(n), :], far_sem, 0, 1, z_up) for n in (3, 2)]
+    far_dn = [remote(grid.at[3, part(n), :], grid.at[2, part(n), :], far_sem, 2, 3, z_dn) for n in (1, 0)]
+    far_all = [
+        remote(grid.at[1, high, :], grid.at[2, high, :], far_sem, 0, 1, z_up),
+        remote(grid.at[3, low, :], grid.at[2, low, :], far_sem, 2, 3, z_dn),
+    ]
+    halo_copy = remote(raw.at[pl.ds(FD - 16, 16), :], halo, halo_sem, 0, 1, nxt)
+    fut_copy = remote(grid.at[0, pl.ds(0, 16), :], fut, fut_sem, 0, 1, prv)
+    asks = [remote(want, asked.at[d], ask_sem, 0, 1, x_of[(4 - d) % 4]) for d in range(1, 4)]
+    asks_all = remote(asked.at[pl.ds(1, 3)], asked.at[pl.ds(1, 3)], ask_sem, 0, 1, x_of[1])
 
     edges = jnp.where(c == 1, jnp.where(has_next, 1, 0), jnp.where(has_prev, 1, 0))
     pl.semaphore_wait(barrier, 12 + edges)
@@ -136,13 +144,14 @@
     spot = [jnp.sum(hit[j] * (rel_rows * SLOT + rank), axis=0, keepdims=True) for j in range(NNEG)]
     code = jnp.where(named > 0, rank, -1)
     slot_rows = iota((SLOT, FD), 0)
-    slot_lane = iota((SLOT, FD), 1)
-    wanted = jnp.zeros((SLOT, FD), I32)
+    pad_rows = iota((PAD, FD), 0)
+    pad_lane = iota((PAD, FD), 1)
+    wanted = jnp.zeros((PAD, FD), I32)
     for r in range(1, 16):
         column = jnp.sum(
-            jnp.where(slot_rows == code[r : r + 1, :], frame_of[r : r + 1, :].astype(F32), 0.0), axis=1, keepdims=True
+            jnp.where(pad_rows == code[r : r + 1, :], frame_of[r : r + 1, :].astype(F32), 0.0), axis=1, keepdims=True
         )
-        wanted = jnp.where(slot_lane == r, column.astype(I32), wanted)
+        wanted = jnp.where(pad_lane == r, column.astype(I32), wanted)
     want[...] = wanted
     for copy in asks:
         copy.start()
@@ -188,7 +197,7 @@
         weighted = (key.astype(F32) * to_end).astype(BF16)
         st_out[h, pl.ds(0, DV), :] = nn(value_t[h], weighted)
         st_out[h, pl.ds(DV, 8), :] = jnp.broadcast_to(total_row[h : h + 1, :], (8, FD))
-    pair_copy = remote(st_out.at[pl.ds(4 - 4 * c, 4)], st_in, pair_sem, (0,), pair)
+    pair_copy = remote(st_out.at[pl.ds(4 - 4 * c, 4)], st_in, pair_sem, 0, 1, pair)
     pair_copy.start()
 
     loads[6].wait()
@@ -211,13 +220,15 @@
         pieces = jnp.where(rows16 == 0, hi, jnp.where(rows16 == 1, mid, jnp.where(rows16 == 2, lo, 0.0)))
         msg_out[n, pl.ds(0, DV), :] = joined.astype(BF16)
         msg_out[n, pl.ds(DV, 16), :] = pieces.astype(BF16)
-    msgs = [remote(msg_out.at[(zl + d) % 4], msg_in.at[zl], msg_sem, (d,), row_of[d]) for d in range(1, 4)]
+    msgs = [remote(msg_out.at[(zl + d) % 4], msg_in.at[zl], msg_sem, 0, 1, row_of[d]) for d in range(1, 4)]
+    msgs_all = remote(msg_out.at[pl.ds(0, 3)], msg_in.at[pl.ds(0, 3)], msg_sem, 0, 1, row_of[1])
     for copy in msgs:
         copy.start()
     msg_in[zl] = msg_out[zl]
-    for n in range(2, 4):
-        up[up_order[n]].start()
-        dn[dn_order[n]].start()
+    up[1].start()
+    dn[3].start()
+    up[0].start()
+    dn[2].start()
 
     scale = 1.0 / math.sqrt(DK)
     for h in range(H):
@@ -228,37 +239,31 @@
         probs_t = (nt(key, query) * weight * scale).astype(BF16)
         inside[h] = nn(value_t[h], probs_t)
 
-    for copy in asks:
-        copy.wait()
+    asks_all.wait()
+
+    for dz in range(4):
+        for d in range(4):
+            lists = want[...] if d == 0 else asked[d]
+            column = jnp.broadcast_to(lists[:, dz * 4 + d : dz * 4 + d + 1], (PAD, FD))
+            chosen[dz, pl.ds(d * PAD, PAD), :] = jnp.where(pad_lane == column, 1.0, 0.0).astype(BF16)
 
     def serve(dz):
-        block = grid[dz]
-        sends = []
-        for d in range(4):
-            if dz == 0 and d == 0:
-                continue
-            lists = want[...] if d == 0 else asked[d]
-            column = jnp.broadcast_to(lists[:, dz * 4 + d : dz * 4 + d + 1], (SLOT, FD))
-            chosen = jnp.where(slot_lane == column, 1.0, 0.0).astype(BF16)
-            got = nn(chosen, block).astype(BF16)
-            if d == 0:
-                rows[dz * 4] = got
-            else:
-                pick[dz, d] = got
-                copy = remote(pick.at[dz, d], rows.at[dz * 4 + d], row_sem, (dz, d), x_of[d])
-                copy.start()
-                sends.append(copy)
-        return sends
+        got = nn(chosen[dz], grid[dz]).astype(BF16)
+        for d in (2, 1, 3):
+            pick[dz, d] = got[d * PAD : d * PAD + SLOT, :]
+            remote(pick.at[dz, d], rows.at[dz * 4 + d], row_sem, dz, 4 + dz, x_of[d]).start()
+        if dz > 0:
+            rows[dz * 4] = got[:SLOT, :]
+        return remote(pick.at[dz, pl.ds(1, 3)], rows.at[pl.ds(dz * 4 + 1, 3)], row_sem, dz, 4 + dz, x_of[1])
 
     sends = {0: serve(0)}
 
-    up[3].wait()
+    up[3].wait_recv()
     far_up[0].start()
-    dn[1].wait()
+    dn[1].wait_recv()
     far_dn[0].start()
 
-    for copy in msgs:
-        copy.wait()
+    msgs_all.wait()
     lam = [jnp.sum(msg_in[n, pl.ds(DV, 16), :].astype(F32), axis=0, keepdims=True) for n in range(4)]
     prefix, reach = [jnp.zeros((DV, FD), F32)], [jnp.zeros((1, FD), F32)]
     for n in range(4):
@@ -266,44 +271,43 @@
         reach.append(reach[-1] + lam[n])
     y_out[pl.ds(0, DV), :] = prefix[4]
     y_out[pl.ds(DV, 8), :] = jnp.broadcast_to(reach[4], (8, FD))
-    y_copies = [remote(y_out, y_in.at[(4 - d) % 4], y_sem, (d,), y_of[d]) for d in range(1, 4)]
+    y_copies = [remote(y_out, y_in.at[(4 - d) % 4], y_sem, 0, 1, y_of[d]) for d in range(1, 4)]
+    y_all = remote(y_in.at[pl.ds(1, 3)], y_in.at[pl.ds(1, 3)], y_sem, 0, 1, y_of[1])
     for copy in y_copies:
         copy.start()
-
-    up[2].wait()
+    up[2].wait_recv()
     far_up[1].start()
-    dn[0].wait()
+    dn[0].wait_recv()
     far_dn[1].start()
 
-    for copy in y_copies:
-        copy.wait()
+    y_all.wait()
     carry = jnp.zeros((DV, FD), F32)
     for d in range(1, 4):
         step = jnp.exp(y_in[d, pl.ds(DV, 1), :]) * carry + y_in[d, pl.ds(0, DV), :]
         carry = jnp.where(d >= 4 - y, step, carry)
     for n in range(4):
         ent_out[n] = (prefix[n] + jnp.exp(reach[n]) * carry).astype(BF16)
-    entries = [remote(ent_out.at[(zl + d) % 4], ent_in.at[zl], ent_sem, (d,), row_of[d]) for d in range(1, 4)]
+    entries = [remote(ent_out.at[(zl + d) % 4], ent_in.at[zl], ent_sem, 0, 1, row_of[d]) for d in range(1, 4)]
+    entries_all = remote(ent_out.at[pl.ds(0, 3)], ent_in.at[pl.ds(0, 3)], ent_sem, 0, 1, row_of[1])
     for copy in entries:
         copy.start()
     ent_in[zl] = ent_out[zl]
 
-    for n in range(2):
-        up[n].wait()
+    up_rest.wait_recv()
     sends[1] = serve(1)
-    for n in range(2, 4):
-        dn[n].wait()
+    dn_rest.wait_recv()
     sends[3] = serve(3)
-
-    for copy in entries:
+    for copy in far_all:
         copy.wait()
+    sends[2] = serve(2)
+    entries_all.wait()
     for n in range(4):
         early, _ = core_states(n)
         at_first = ent_in[n].astype(F32)
         at_second = jnp.exp(early[DV : DV + 1, :]) * at_first + early[:DV, :]
         ent[4 * c + n] = jnp.where(c == 0, at_first, at_second).astype(BF16)
         ent_pair[n] = jnp.where(c == 0, at_second, at_first).astype(BF16)
-    back_copy = remote(ent_pair, ent.at[pl.ds(4 * c, 4)], pair_sem, (1,), pair)
+    back_copy = remote(ent_pair, ent.at[pl.ds(4 * c, 4)], pair_sem, 2, 3, pair)
     back_copy.start()
     loads[7].wait()
     back_copy.wait()
@@ -330,10 +334,6 @@
     def _():
         fut[...] = jnp.zeros_like(fut)
 
-    for copy in far_up + far_dn:
-        copy.wait()
-    sends[2] = serve(2)
-
     inv_width = 1.0 / math.sqrt(E)
     valid_lane = jnp.where(lane[0:1, :] + m * FD < length, inv_width, 0.0)
     later = iota((16, FD), 0) + FD
@@ -358,9 +358,10 @@
                     negative[k][j] += jnp.sum(jnp.where(found[j], scores, 0.0), axis=0, keepdims=True)
 
     for dz in (0, 1, 3, 2):
-        for copy in sends[dz]:
-            copy.wait()
+        sends[dz].wait()
         score(dz)
+    up_all.wait_send()
+    dn_all.wait_send()
     for k in range(K):
         for j in range(NNEG):
             out_ref[0, k, 1 + j : 2 + j, :] = negative[k][j] * valid_lane
@@ -371,7 +372,7 @@
     dma = pltpu.SemaphoreType.DMA
     return pl.pallas_call(
         kernel,
-        out_shape=jax.ShapeDtypeStruct((1, K, 1 + NNEG, FD), F32),
+        out_shape=pltpu.VMEM((1, K, 1 + NNEG, FD), F32),
         in_specs=[hbm] * 8 + [pl.BlockSpec(memory_space=pltpu.SMEM)],
         out_specs=pl.BlockSpec(memory_space=pltpu.VMEM),
         scratch_shapes=[
@@ -385,11 +386,12 @@
             pltpu.VMEM((NNEG, 1, FD), I32),
             pltpu.VMEM((16, FRAME_W), BF16),
             pltpu.VMEM((16, E), BF16),
-            pltpu.VMEM((SLOT, FD), I32),
-            pltpu.VMEM((4, SLOT, FD), I32),
+            pltpu.VMEM((PAD, FD), I32),
+            pltpu.VMEM((4, PAD, FD), I32),
             pltpu.VMEM((4, FD, E), BF16),
             pltpu.VMEM((4, 4, SLOT, E), BF16),
             pltpu.VMEM((16, SLOT, E), BF16),
+            pltpu.VMEM((4, 4 * PAD, FD), BF16),
             pltpu.VMEM((H, DV + 8, FD), F32),
             pltpu.VMEM((4, DV + 8, FD), F32),
             pltpu.VMEM((4, MSG, FD), BF16),
@@ -405,14 +407,14 @@
             dma((8,)),
             dma((2,)),
             dma((2,)),
-            dma((2, 4)),
-            dma((2, 2, 4)),
-            dma((2, 2, 2)),
-            dma((2, 4, 4)),
-            dma((2, 2)),
-            dma((2, 4)),
-            dma((2, 4)),
-            dma((2, 4)),
+            dma((2,)),
+            dma((8,)),
+            dma((4,)),
+            dma((8,)),
+            dma((4,)),
+            dma((2,)),
+            dma((2,)),
+            dma((2,)),
         ],
         compiler_params=pltpu.CompilerParams(collective_id=0, has_side_effects=True),
     )(

time: 49.2 us -> 44.1 us (0.90)
  the two profiles are of different devices: /device:TPU:1 before, /device:TPU:48 now
where the time goes in v3:
time: 44.1 us; the launch traced here: 44 us
  Pallas kernels  42.7 us (97%)
  between operations  0.66 us (1%)
  local copies, waits for them, and re-layouts  0.6 us (1%)
    pallas_call x1, Pallas kernels, shards(): pl.pallas_call(kernel, out_shape=pltpu.VMEM((1, K, 1 + NNEG, FD), F32), i...  42.7 us

profile of v3, /device:TPU:48, one launch (start us, length us, event | category | flops | bytes accessed | tf_op | source)
XLA Modules:
  0.0 44.0 jit_solution(18138224359219404254)
XLA Ops:
  0.7 42.7 %shard_map.91 = f32[1,2,4,128]{3,2,1,0:T(4,128)S(1)} custom-call(bf16[1,128,640]{2,1,0:T(8,128)(2,1)} %raw_hbm.1, bf16[1280,512]{1,0:T(8,128)(2,1)} %wc_hbm.1, bf16[512,1024]{1,0:T(8,128)(2,1)} %wq_hbm.1, bf16[512,1024]{1,0:T(8,128)(2,1)} %wk_hbm.1, bf16[2,512,512]{2,1,0:T(8,128)(2,1)} %wp_hbm.1, f32[1,8,128]{2,1,0:T(8,128)} %ld_hbm.1, ...), custom_call_target="tpu_custom_call" | custom-call | tf_op jit(solution)/shard_map/pallas_call | solution.py:373
  43.4 0.6 %copy.11 = f32[1,2,4,128]{3,2,1,0:T(4,128)} copy(f32[1,2,4,128]{3,2,1,0:T(4,128)S(1)} %shard_map.91) | data formatting | bytes 8192

commit v4 on v3

--- a/solution.py
+++ b/solution.py
@@ -14,7 +14,8 @@
 DK, DV = DA // H, E // H
 SLOT, PAD = 40, 48
 CHUNK = FD // 4
-MSG = DV + 16
+BASE = (0, 4, 12, 8)
+MSG = DV + 8
 YMSG = DV + 8
 
 
@@ -80,6 +81,9 @@
 
     for load in loads[2:]:
         load.start()
+
+    for n in range(1, 16):
+        rows[n, pl.ds(SLOT, PAD - SLOT), :] = jnp.zeros((PAD - SLOT, E), BF16)
 
     lane = iota((FD, FD), 1)
     sub = iota((FD, FD), 0)
@@ -133,7 +137,8 @@
     rel_j, frame_j = [], []
     for j in range(NNEG):
         group = (b + off[j] + 1) & 15
-        rel_j.append((((zh - (group >> 2)) & 3) << 2) | ((x - (group & 3)) & 3))
+        dz = (zh - (group >> 2)) & 3
+        rel_j.append(((dz ^ (dz >> 1)) << 2) | ((x - (group & 3)) & 3))
         frame_j.append(frm[j])
     rel_rows = iota((16, FD), 0)
     hit = [jnp.where(rel_rows == rel_j[j], 1, 0) for j in range(NNEG)]
@@ -141,9 +146,8 @@
     frame_of = hit[0] * frame_j[0] + hit[1] * frame_j[1] + hit[2] * frame_j[2]
     upto = jnp.where(sub <= lane, 1.0, 0.0).astype(BF16)
     rank = nn(named.astype(F32).astype(BF16), upto).astype(I32) - 1
-    spot = [jnp.sum(hit[j] * (rel_rows * SLOT + rank), axis=0, keepdims=True) for j in range(NNEG)]
+    spot = [jnp.sum(hit[j] * (rel_rows * PAD + rank), axis=0, keepdims=True) for j in range(NNEG)]
     code = jnp.where(named > 0, rank, -1)
-    slot_rows = iota((SLOT, FD), 0)
     pad_rows = iota((PAD, FD), 0)
     pad_lane = iota((PAD, FD), 1)
     wanted = jnp.zeros((PAD, FD), I32)
@@ -209,7 +213,7 @@
         return jnp.where(c == 0, own, other), jnp.where(c == 0, other, own)
 
     pair_copy.wait()
-    rows16 = iota((16, FD), 0)
+    piece = iota((8, FD), 0)
     for n in range(4):
         early, late = core_states(n)
         joined = jnp.exp(late[DV : DV + 1, :]) * early[:DV, :] + late[:DV, :]
@@ -217,9 +221,9 @@
         hi = whole.astype(BF16).astype(F32)
         mid = (whole - hi).astype(BF16).astype(F32)
         lo = whole - hi - mid
-        pieces = jnp.where(rows16 == 0, hi, jnp.where(rows16 == 1, mid, jnp.where(rows16 == 2, lo, 0.0)))
+        pieces = jnp.where(piece == 0, hi, jnp.where(piece == 1, mid, jnp.where(piece == 2, lo, 0.0)))
         msg_out[n, pl.ds(0, DV), :] = joined.astype(BF16)
-        msg_out[n, pl.ds(DV, 16), :] = pieces.astype(BF16)
+        msg_out[n, pl.ds(DV, 8), :] = pieces.astype(BF16)
     msgs = [remote(msg_out.at[(zl + d) % 4], msg_in.at[zl], msg_sem, 0, 1, row_of[d]) for d in range(1, 4)]
     msgs_all = remote(msg_out.at[pl.ds(0, 3)], msg_in.at[pl.ds(0, 3)], msg_sem, 0, 1, row_of[1])
     for copy in msgs:
@@ -244,17 +248,17 @@
     for dz in range(4):
         for d in range(4):
             lists = want[...] if d == 0 else asked[d]
-            column = jnp.broadcast_to(lists[:, dz * 4 + d : dz * 4 + d + 1], (PAD, FD))
+            column = jnp.broadcast_to(lists[:, BASE[dz] + d : BASE[dz] + d + 1], (PAD, FD))
             chosen[dz, pl.ds(d * PAD, PAD), :] = jnp.where(pad_lane == column, 1.0, 0.0).astype(BF16)
 
     def serve(dz):
         got = nn(chosen[dz], grid[dz]).astype(BF16)
         for d in (2, 1, 3):
             pick[dz, d] = got[d * PAD : d * PAD + SLOT, :]
-            remote(pick.at[dz, d], rows.at[dz * 4 + d], row_sem, dz, 4 + dz, x_of[d]).start()
+            remote(pick.at[dz, d], rows.at[BASE[dz] + d, pl.ds(0, SLOT), :], row_sem, dz, 4 + dz, x_of[d]).start()
         if dz > 0:
-            rows[dz * 4] = got[:SLOT, :]
-        return remote(pick.at[dz, pl.ds(1, 3)], rows.at[pl.ds(dz * 4 + 1, 3)], row_sem, dz, 4 + dz, x_of[1])
+            rows[BASE[dz], pl.ds(0, SLOT), :] = got[:SLOT, :]
+        return remote(pick.at[dz, pl.ds(1, 3)], rows.at[pl.ds(BASE[dz] + 1, 3), pl.ds(0, SLOT), :], row_sem, dz, 4 + dz, x_of[1])
 
     sends = {0: serve(0)}
 
@@ -264,7 +268,7 @@
     far_dn[0].start()
 
     msgs_all.wait()
-    lam = [jnp.sum(msg_in[n, pl.ds(DV, 16), :].astype(F32), axis=0, keepdims=True) for n in range(4)]
+    lam = [jnp.sum(msg_in[n, pl.ds(DV, 8), :].astype(F32), axis=0, keepdims=True) for n in range(4)]
     prefix, reach = [jnp.zeros((DV, FD), F32)], [jnp.zeros((1, FD), F32)]
     for n in range(4):
         prefix.append(jnp.exp(lam[n]) * prefix[-1] + msg_in[n, pl.ds(0, DV), :].astype(F32))
@@ -309,6 +313,19 @@
         ent_pair[n] = jnp.where(c == 0, at_second, at_first).astype(BF16)
     back_copy = remote(ent_pair, ent.at[pl.ds(4 * c, 4)], pair_sem, 2, 3, pair)
     back_copy.start()
+    @pl.when(has_prev)
+    def _():
+        fut_copy.wait_send()
+
+    @pl.when(has_next)
+    def _():
+        fut_copy.wait_recv()
+        halo_copy.wait_send()
+
+    @pl.when(jnp.logical_not(has_next))
+    def _():
+        fut[...] = jnp.zeros_like(fut)
+
     loads[7].wait()
     back_copy.wait()
     halves = []
@@ -321,50 +338,42 @@
     )
     predicted = [nn(context, wp[k]).astype(BF16) for k in range(K)]
 
-    @pl.when(has_prev)
-    def _():
-        fut_copy.wait_send()
-
-    @pl.when(has_next)
-    def _():
-        fut_copy.wait_recv()
-        halo_copy.wait_send()
-
-    @pl.when(jnp.logical_not(has_next))
-    def _():
-        fut[...] = jnp.zeros_like(fut)
-
+    for dz in (0, 1, 3):
+        sends[dz].wait()
+    predicted = jnp.concatenate(predicted, axis=0)
     inv_width = 1.0 / math.sqrt(E)
     valid_lane = jnp.where(lane[0:1, :] + m * FD < length, inv_width, 0.0)
     later = iota((16, FD), 0) + FD
     later_lane = iota((16, FD), 1)
+    here, ahead = nt(grid[0], predicted), nt(fut[...], predicted)
     for k in range(K):
-        here = jnp.where(sub == lane + (k + 1), nt(grid[0], predicted[k]), 0.0)
-        ahead = jnp.where(later == later_lane + (k + 1), nt(fut[...], predicted[k]), 0.0)
-        positive = jnp.sum(here, axis=0, keepdims=True) + jnp.sum(ahead, axis=0, keepdims=True)
+        span = slice(k * FD, (k + 1) * FD)
+        positive = jnp.sum(jnp.where(sub == lane + (k + 1), here[:, span], 0.0), axis=0, keepdims=True) + jnp.sum(
+            jnp.where(later == later_lane + (k + 1), ahead[:, span], 0.0), axis=0, keepdims=True
+        )
         out_ref[0, k, 0:1, :] = positive * valid_lane
 
     negative = [[jnp.zeros((1, FD), F32) for _ in range(NNEG)] for _ in range(K)]
 
-    def score(dz):
-        start = 1 if dz == 0 else 0
-        for d in range(start, 4):
-            n = dz * 4 + d
-            block = rows[n]
-            found = [slot_rows + n * SLOT == spot[j] for j in range(NNEG)]
+    def score(start, stop):
+        count = (stop - start) * PAD
+        scores = nt(rows[pl.ds(start, stop - start)].reshape(count, E), predicted)
+        place = iota((count, FD), 0) + start * PAD
+        for j in range(NNEG):
+            found = place == spot[j]
             for k in range(K):
-                scores = nt(block, predicted[k])
-                for j in range(NNEG):
-                    negative[k][j] += jnp.sum(jnp.where(found[j], scores, 0.0), axis=0, keepdims=True)
-
-    for dz in (0, 1, 3, 2):
-        sends[dz].wait()
-        score(dz)
-    up_all.wait_send()
-    dn_all.wait_send()
+                negative[k][j] += jnp.sum(
+                    jnp.where(found, scores[:, k * FD : (k + 1) * FD], 0.0), axis=0, keepdims=True
+                )
+
+    score(1, 12)
+    sends[2].wait()
+    score(12, 16)
     for k in range(K):
         for j in range(NNEG):
             out_ref[0, k, 1 + j : 2 + j, :] = negative[k][j] * valid_lane
+    up_all.wait_send()
+    dn_all.wait_send()
 
 
 def shards(raw, w_conv, w_query, w_key, w_pred, log_decay, lengths, neg_offset, neg_frame):
@@ -390,7 +399,7 @@
             pltpu.VMEM((4, PAD, FD), I32),
             pltpu.VMEM((4, FD, E), BF16),
             pltpu.VMEM((4, 4, SLOT, E), BF16),
-            pltpu.VMEM((16, SLOT, E), BF16),
+            pltpu.VMEM((16, PAD, E), BF16),
             pltpu.VMEM((4, 4 * PAD, FD), BF16),
             pltpu.VMEM((H, DV + 8, FD), F32),
             pltpu.VMEM((4, DV + 8, FD), F32),

time: 44.1 us -> 42.6 us (0.966)
  the two profiles are of different devices: /device:TPU:48 before, /device:TPU:40 now
where the time goes in v4:
time: 42.6 us; the launch traced here: 42.5 us
  Pallas kernels  41.2 us (97%)
  between operations  0.66 us (2%)
  local copies, waits for them, and re-layouts  0.6 us (1%)
    pallas_call x1, Pallas kernels, shards(): pl.pallas_call(kernel, out_shape=pltpu.VMEM((1, K, 1 + NNEG, FD), F32), i...  41.2 us

profile of v4, /device:TPU:40, one launch (start us, length us, event | category | flops | bytes accessed | tf_op | source)
XLA Modules:
  0.0 42.5 jit_solution(14450631645250832075)
XLA Ops:
  0.7 41.2 %shard_map.91 = f32[1,2,4,128]{3,2,1,0:T(4,128)S(1)} custom-call(bf16[1,128,640]{2,1,0:T(8,128)(2,1)} %raw_hbm.1, bf16[1280,512]{1,0:T(8,128)(2,1)} %wc_hbm.1, bf16[512,1024]{1,0:T(8,128)(2,1)} %wq_hbm.1, bf16[512,1024]{1,0:T(8,128)(2,1)} %wk_hbm.1, bf16[2,512,512]{2,1,0:T(8,128)(2,1)} %wp_hbm.1, f32[1,8,128]{2,1,0:T(8,128)} %ld_hbm.1, ...), custom_call_target="tpu_custom_call" | custom-call | tf_op jit(solution)/shard_map/pallas_call | solution.py:382
  41.9 0.6 %copy.11 = f32[1,2,4,128]{3,2,1,0:T(4,128)} copy(f32[1,2,4,128]{3,2,1,0:T(4,128)S(1)} %shard_map.91) | data formatting | bytes 8192

commit v5 on v4

--- a/solution.py
+++ b/solution.py
@@ -109,8 +109,13 @@
     up = [remote(grid.at[0, part(n), :], grid.at[1, part(n), :], near_sem, 0, 2 + max(n - 1, 0), z_up) for n in range(4)]
     dn = [remote(grid.at[0, part(n), :], grid.at[3, part(n), :], near_sem, 1, 5 + min(n, 2), z_dn) for n in range(4)]
     up_all, dn_all = remote(grid.at[0], grid.at[1], near_sem, 0, 2, z_up), remote(grid.at[0], grid.at[3], near_sem, 1, 7, z_dn)
-    up_rest = remote(grid.at[0, low, :], grid.at[1, low, :], near_sem, 0, 2, z_up)
-    dn_rest = remote(grid.at[0, high, :], grid.at[3, high, :], near_sem, 1, 7, z_dn)
+    near_1 = jnp.where(zl < 2, 3, 1)
+    near_3 = 4 - near_1
+
+    def rest(dz):
+        half = pl.ds(pl.multiple_of((dz // 2) * 2 * CHUNK, 2 * CHUNK), 2 * CHUNK)
+        return remote(grid.at[0, half, :], grid.at[dz, half, :], near_sem, dz // 2, 2 + (dz // 2) * 5, z_up)
+
     far_up = [remote(grid.at[1, part(n), :], grid.at[2, part(n), :], far_sem, 0, 1, z_up) for n in (3, 2)]
     far_dn = [remote(grid.at[3, part(n), :], grid.at[2, part(n), :], far_sem, 2, 3, z_dn) for n in (1, 0)]
     far_all = [
@@ -231,8 +236,6 @@
     msg_in[zl] = msg_out[zl]
     up[1].start()
     dn[3].start()
-    up[0].start()
-    dn[2].start()
 
     scale = 1.0 / math.sqrt(DK)
     for h in range(H):
@@ -243,6 +246,9 @@
         probs_t = (nt(key, query) * weight * scale).astype(BF16)
         inside[h] = nn(value_t[h], probs_t)
 
+    up[0].start()
+    dn[2].start()
+
     asks_all.wait()
 
     for dz in range(4):
@@ -251,16 +257,18 @@
             column = jnp.broadcast_to(lists[:, BASE[dz] + d : BASE[dz] + d + 1], (PAD, FD))
             chosen[dz, pl.ds(d * PAD, PAD), :] = jnp.where(pad_lane == column, 1.0, 0.0).astype(BF16)
 
-    def serve(dz):
+    def serve(dz, base):
         got = nn(chosen[dz], grid[dz]).astype(BF16)
         for d in (2, 1, 3):
             pick[dz, d] = got[d * PAD : d * PAD + SLOT, :]
-            remote(pick.at[dz, d], rows.at[BASE[dz] + d, pl.ds(0, SLOT), :], row_sem, dz, 4 + dz, x_of[d]).start()
-        if dz > 0:
-            rows[BASE[dz], pl.ds(0, SLOT), :] = got[:SLOT, :]
-        return remote(pick.at[dz, pl.ds(1, 3)], rows.at[pl.ds(BASE[dz] + 1, 3), pl.ds(0, SLOT), :], row_sem, dz, 4 + dz, x_of[1])
-
-    sends = {0: serve(0)}
+            remote(pick.at[dz, d], rows.at[base + d, pl.ds(0, SLOT), :], row_sem, dz, 4 + dz, x_of[d]).start()
+        if base is not BASE[0]:
+            rows[base, pl.ds(0, SLOT), :] = got[:SLOT, :]
+        return remote(
+            pick.at[dz, pl.ds(1, 3)], rows.at[pl.ds(base + 1, 3), pl.ds(0, SLOT), :], row_sem, dz, 4 + dz, x_of[1]
+        )
+
+    sends = {0: serve(0, BASE[0])}
 
     up[3].wait_recv()
     far_up[0].start()
@@ -297,13 +305,13 @@
         copy.start()
     ent_in[zl] = ent_out[zl]
 
-    up_rest.wait_recv()
-    sends[1] = serve(1)
-    dn_rest.wait_recv()
-    sends[3] = serve(3)
+    rest(near_1).wait_recv()
+    sends[1] = serve(near_1, 2 * near_1 + 2)
+    rest(near_3).wait_recv()
+    sends[3] = serve(near_3, 2 * near_3 + 2)
     for copy in far_all:
         copy.wait()
-    sends[2] = serve(2)
+    sends[2] = serve(2, BASE[2])
     entries_all.wait()
     for n in range(4):
         early, _ = core_states(n)

time: 42.6 us -> 41.7 us (0.979)
  the two profiles are of different devices: /device:TPU:40 before, /device:TPU:1 now
where the time goes in v5:
time: 41.7 us; the launch traced here: 41.3 us
  Pallas kernels  40 us (96%)
  between operations  0.66 us (2%)
  local copies, waits for them, and re-layouts  0.6 us (1%)
    pallas_call x1, Pallas kernels, shards(): pl.pallas_call(kernel, out_shape=pltpu.VMEM((1, K, 1 + NNEG, FD), F32), i...  40 us

profile of v5, /device:TPU:1, one launch (start us, length us, event | category | flops | bytes accessed | tf_op | source)
XLA Modules:
  0.0 41.3 jit_solution(2390754864783980787)
XLA Ops:
  0.7 40.0 %shard_map.91 = f32[1,2,4,128]{3,2,1,0:T(4,128)S(1)} custom-call(bf16[1,128,640]{2,1,0:T(8,128)(2,1)} %raw_hbm.1, bf16[1280,512]{1,0:T(8,128)(2,1)} %wc_hbm.1, bf16[512,1024]{1,0:T(8,128)(2,1)} %wq_hbm.1, bf16[512,1024]{1,0:T(8,128)(2,1)} %wk_hbm.1, bf16[2,512,512]{2,1,0:T(8,128)(2,1)} %wp_hbm.1, f32[1,8,128]{2,1,0:T(8,128)} %ld_hbm.1, ...), custom_call_target="tpu_custom_call" | custom-call | tf_op jit(solution)/shard_map/pallas_call | solution.py:390
  40.7 0.6 %copy.11 = f32[1,2,4,128]{3,2,1,0:T(4,128)} copy(f32[1,2,4,128]{3,2,1,0:T(4,128)S(1)} %shard_map.91) | data formatting | bytes 8192
